TPU v7x, 128 devices: a whole 4x4x4 slice. The times are simulated.
128 devices in a mesh: ctx: 32 (over x, z, core), head: 4 (over y).
Axes of the slice: x: 4, y: 4, z: 4, core: 2. Of those that a mesh axis runs over, the one named last changes fastest.
Arguments:
- query_raw: bfloat16 [32768, 2048], P('ctx', 'head'), may hold values from -6 to 6
- key_raw: bfloat16 [32768, 2048], P('ctx', 'head'), may hold values from -6 to 6
- value_raw: bfloat16 [32768, 4096], P('ctx', 'head'), may hold values from -6 to 6
- gate_branch: bfloat16 [32768, 4096], P('ctx', 'head'), may hold values from -6 to 6
- gate_code: int32 [32768, 32], P('ctx', 'head'), may hold values from 0 to 1000
- beta_code: int32 [32768, 32], P('ctx', 'head'), may hold values from 0 to 1000
- conv_query: bfloat16 [4, 2048], P(None, 'head'), may hold values from -3 to 3
- conv_key: bfloat16 [4, 2048], P(None, 'head'), may hold values from -3 to 3
- conv_value: bfloat16 [4, 4096], P(None, 'head'), may hold values from -3 to 3
- norm_gain: float32 [128], replicated, may hold values from 0.1 to 1.9
- out_weight: bfloat16 [4096, 2048], P('head'), may hold values from -0.09375 to 0.09375
Outputs:
- layer_out: bfloat16 [32768, 2048], P(('ctx', 'head'))
All inputs are finite; a program needn't handle non-finite values.
Results may differ from a plain program's by a relative error of at most 0.002.
The roundings to bfloat16 on the way count: a program that leaves them out, or rounds other values in their place, can miss the bound.
Values may be sent and summed in bfloat16 or wider, within the bound.
No kernel may reach another device: no remote copies, remote signals or barrier semaphores. Data moves between devices by JAX's collectives and lax.ppermute only.
A program may use at most 128 MiB of HBM per device.

v0:
```python
import functools

import jax, jax.numpy as jnp
from jax import lax
from jax.experimental import pallas as pl
from jax.experimental.pallas import tpu as pltpu
from jax.sharding import PartitionSpec as P


Z_CHIPS, X_CHIPS, CORES = 4, 4, 2

F32, BF16 = jnp.float32, jnp.bfloat16
HD = 128
BLOCK = 64
KERNEL = 4
LIMIT = 12 << 20


def split(x):
    hi = x.astype(BF16)
    return hi, (x - hi.astype(F32)).astype(BF16)


def mxu(a, b):
    return jnp.dot(a, b, preferred_element_type=F32)


def cat(parts, axis):
    return jnp.concatenate(parts, axis)


def silu(x):
    return x / (1.0 + jnp.exp(-x))


def pair_rhs(y, left):
    hi, lo = split(y)
    zero = jnp.zeros_like(hi)
    hi = cat([jnp.where(left, hi, zero), jnp.where(left, zero, hi)], 0)
    lo = cat([jnp.where(left, lo, zero), jnp.where(left, zero, lo)], 0)
    row = cat([hi, lo], 1)
    return cat([row, row], 0)


def wide(x):
    return cat(split(x), 1)


def fold(out):
    return out[:, :HD] + out[:, HD:]


def pair_inverses(lows, eye, left, fills):
    raw = [mxu(wide(low), pair_rhs(low, left)) for low in lows]
    fills[0]()
    powers = [fold(r) for r in raw]
    invs = [eye - low for low in lows]
    for fill in fills[1:-1]:
        raw = [mxu(wide(cat([i, p], 0)), pair_rhs(p, left)) for i, p in zip(invs, powers)]
        fill()
        outs = [fold(r) for r in raw]
        invs = [i + o[:BLOCK] for i, o in zip(invs, outs)]
        powers = [o[BLOCK:] for o in outs]
    raw = [mxu(wide(i), pair_rhs(p, left)) for i, p in zip(invs, powers)]
    fills[-1]()
    return [i + fold(r) for i, r in zip(invs, raw)]


def conv(ext, taps):
    acc = None
    for j in range(KERNEL):
        s = KERNEL - 1 - j
        shifted = ext if s == 0 else pltpu.roll(ext, s, 0)
        term = taps[j : j + 1] * shifted[8:]
        acc = term if acc is None else acc + term
    return silu(acc)


def unit(x):
    return x * lax.rsqrt(jnp.sum(x * x, -1, keepdims=True) + 1e-06)


def scan_kernel(pos, q_ref, k_ref, v_ref, gc_ref, bc_ref, halo_ref, cq_ref, ck_ref, cv_ref,
                base_ref, map_ref, kept_ref, away_ref, state, carry, codes):
    n = pl.program_id(0)
    kh = q_ref.shape[1] // HD
    vh = v_ref.shape[1] // HD
    kw = kh * HD

    @pl.when(n == 0)
    def _():
        carry[...] = halo_ref[...].astype(F32)
        codes[0] = jnp.transpose(gc_ref[...].astype(F32))
        codes[1] = jnp.transpose(bc_ref[...].astype(F32))
        r = lax.broadcasted_iota(jnp.int32, (HD, 2 * HD), 0)
        c = lax.broadcasted_iota(jnp.int32, (HD, 2 * HD), 1)
        start = jnp.where(r + HD == c, 1.0, 0.0).astype(F32)
        for h in range(vh):
            state[h] = start

    rows = lax.broadcasted_iota(jnp.int32, (BLOCK, HD), 0)
    lanes = lax.broadcasted_iota(jnp.int32, (BLOCK, HD), 1)
    left = lanes < BLOCK
    cols = jnp.where(left, lanes, lanes - BLOCK)
    causal = rows >= cols
    strict = rows > cols
    eye = jnp.where(rows == cols, 1.0, 0.0).astype(F32)
    left_t = lax.broadcasted_iota(jnp.int32, (HD, HD), 1) < BLOCK

    here = pl.ds(pl.multiple_of(n * BLOCK, BLOCK), BLOCK)
    log_gate = jnp.log1p(-1e-06 * codes[0, here])
    tri = jnp.where(causal, 1.0, 0.0).astype(F32)[:, :BLOCK]
    cum = jnp.dot(tri, log_gate, precision=lax.Precision.HIGHEST, preferred_element_type=F32)
    gamma = jnp.exp(cum)
    beta = codes[1, here] / 1000.0
    beta_g = beta * jnp.exp(-cum)
    last = gamma[BLOCK - 1 :]

    def conved(ref, taps, src, dst, width):
        x = ref[:, src : src + width].astype(F32)
        ext = cat([carry[:, dst : dst + width], x], 0)
        carry[:, dst : dst + width] = x[BLOCK - 8 :]
        return conv(ext, taps[:, src : src + width].astype(F32))

    pairs = range(kh)
    each = range(vh)
    bs = [jnp.broadcast_to(beta[:, h : h + 1], (BLOCK, HD)) for h in each]
    kt2, k2, q2, lows = [], [], [None] * kh, []
    for j in pairs:
        k = unit(conved(k_ref, ck_ref, j * HD, kw + j * HD, HD))
        kt_hi, kt_lo = split(jnp.transpose(cat([k, k], 0)))
        kt2.append((kt_hi, kt_lo))
        k2.append(wide(k))
    for j in pairs:
        row = cat(kt2[j], 1)
        dots = fold(mxu(k2[j], cat([row, row], 0)))
        lows.append(jnp.where(strict, jnp.where(left, bs[2 * j], bs[2 * j + 1]) * dots, 0.0))
    km4, zs, vs = [None] * kh, [None] * vh, [None] * vh

    def fill_q(js):
        for j in js:
            q2[j] = wide(unit(conved(q_ref, cq_ref, j * HD, j * HD, HD)) * HD ** (-0.5))

    def fill_mix(js):
        for j in js:
            row = cat(kt2[j], 1)
            dots = fold(mxu(q2[j], cat([row, row], 0)))
            mh, ml = split(jnp.where(causal, dots, 0.0))
            km = cat([jnp.where(left_t, *kt2[j]), jnp.where(left, mh, ml)], 0)
            km4[j] = cat([km, km], 1)

    def fill_v(hs):
        for h in hs:
            vs[h] = beta_g[:, h : h + 1] * conved(v_ref, cv_ref, h * HD, 2 * kw + h * HD, HD)

    def fill_z(hs):
        for h in hs:
            s_hi, s_lo = split(state[h])
            kq = cat([k2[h // 2], q2[h // 2]], 0)
            zs[h] = mxu(cat([kq, kq[:, :HD]], 1), cat([s_hi, s_hi, s_lo], 0))

    half = vh // 2
    fills = [lambda: fill_q(pairs[: kh // 2]), lambda: fill_q(pairs[kh // 2 :]), lambda: fill_mix(pairs),
             lambda: fill_v(each[:half]), lambda: fill_v(each[half:]), lambda: fill_z(each)]
    invs = pair_inverses(lows, eye, left, fills)
    ts = []
    for inv in invs:
        ih, il = split(inv)
        rh, rl = split(pltpu.roll(inv, BLOCK, 1))
        for t in (jnp.where(left, ih, rl), jnp.where(left, rh, il)):
            ts.append(cat([t, t], 1))
    us = []
    for h in each:
        z = zs[h]
        right = cat([vs[h] - bs[h] * z[:BLOCK, :HD], -bs[h] * z[:BLOCK, HD:]], 1)
        r_hi, r_lo = split(right)
        us.append(mxu(ts[h], cat([r_hi, r_hi, r_lo, r_lo], 0)))
    for h in each:
        u_hi, u_lo = split(us[h])
        ds = mxu(km4[h // 2], cat([u_hi, u_hi, u_lo, u_lo], 0))
        o = gamma[:, h : h + 1] * (zs[h][BLOCK:] + ds[HD:])
        state[h] = last[:, h : h + 1] * (state[h] + ds[:HD])
        base_ref[here, h * HD : (h + 1) * HD] = o[:, :HD]
        o_hi, o_lo = split(o[:, HD:])
        map_ref[here, 2 * h * HD : (2 * h + 1) * HD] = o_hi
        map_ref[here, (2 * h + 1) * HD : (2 * h + 2) * HD] = o_lo

    @pl.when(n == pl.num_programs(0) - 1)
    def _():
        per = vh // 2
        for i in range(per):
            kept_ref[i] = state[pos[2] * per + i]
            away_ref[i] = state[(1 - pos[2]) * per + i]


def run_scan(pos, q, k, v, gc, bc, halo, cq, ck, cv):
    rows = q.shape[0]
    kw, vw = q.shape[1], v.shape[1]
    vh = vw // HD
    row_spec = lambda w: pl.BlockSpec((BLOCK, w), lambda n: (n, 0))
    full = lambda shape: pl.BlockSpec(shape, lambda n: (0,) * len(shape))
    half = (vh // 2, HD, 2 * HD)
    return pl.pallas_call(
        scan_kernel,
        grid=(rows // BLOCK,),
        in_specs=[pl.BlockSpec(memory_space=pltpu.SMEM), row_spec(kw), row_spec(kw), row_spec(vw),
                  full(gc.shape), full(bc.shape), full(halo.shape), full(cq.shape), full(ck.shape), full(cv.shape)],
        out_specs=[pl.BlockSpec(memory_space=pltpu.VMEM)] * 4,
        out_shape=[jax.ShapeDtypeStruct((rows, vw), F32), jax.ShapeDtypeStruct((rows, 2 * vw), BF16)]
        + [jax.ShapeDtypeStruct(half, F32)] * 2,
        scratch_shapes=[pltpu.VMEM((vh, HD, 2 * HD), F32), pltpu.VMEM((8, 2 * kw + vw), F32),
                        pltpu.VMEM((2, rows, vh), F32)],
        compiler_params=pltpu.CompilerParams(dimension_semantics=("arbitrary",), vmem_limit_bytes=20 << 20),
        name="scan",
    )(pos, q, k, v, gc, bc, halo, cq, ck, cv)


def dot3(a, b):
    a_hi, a_lo = split(a)
    b_hi, b_lo = split(b)
    return mxu(cat([a_hi, a_lo, a_hi], 1), cat([b_hi, b_hi, b_lo], 0))


def then(later, earlier):
    out = dot3(later[:, HD:], earlier)
    return cat([later[:, :HD] + out[:, :HD], out[:, HD:]], 1)


def vmem_call(body, outs, scratch, scalars, *arrays):
    return pl.pallas_call(
        body,
        in_specs=[pl.BlockSpec(memory_space=pltpu.SMEM)] + [pl.BlockSpec(memory_space=pltpu.VMEM)] * len(arrays),
        out_specs=[pl.BlockSpec(memory_space=pltpu.VMEM)] * len(outs),
        out_shape=[jax.ShapeDtypeStruct(s, F32) for s in outs],
        scratch_shapes=[pltpu.VMEM(s, F32) for s in scratch],
        compiler_params=pltpu.CompilerParams(vmem_limit_bytes=LIMIT),
    )(scalars, *arrays)


def pair_kernel(pos, kept, got, early_ref, o0, o1, o2, o3, both):
    first = pos[2] == 0
    for h in range(Z_CHIPS):
        mine, other = kept[h], got[h]
        early = jnp.where(first, mine, other)
        late = jnp.where(first, other, mine)
        early_ref[h] = early
        both[h] = then(late, early)
    for d, o in enumerate((o0, o1, o2, o3)):
        o[...] = both[(pos[1] + d) % Z_CHIPS]


def prefix_kernel(pos, a0, a1, a2, a3, pre_ref, tot_ref, line):
    z = pos[1]
    for d, a in enumerate((a0, a1, a2, a3)):
        line[(z - d + Z_CHIPS) % Z_CHIPS] = a[...]
    r = lax.broadcasted_iota(jnp.int32, (HD, 2 * HD), 0)
    c = lax.broadcasted_iota(jnp.int32, (HD, 2 * HD), 1)
    pre_ref[0] = jnp.where(r + HD == c, 1.0, 0.0).astype(F32)
    lower = line[0]
    middle = then(line[1], lower)
    pre_ref[1] = lower
    pre_ref[2] = middle
    pre_ref[3] = then(line[2], middle)
    tot_ref[...] = then(then(line[3], line[2]), middle)


def entry_kernel(pos, a0, a1, a2, a3, pre, o0, o1, o2, o3, line, states):
    x, z = pos[0], pos[1]
    for d, a in enumerate((a0, a1, a2, a3)):
        line[(x - d + X_CHIPS) % X_CHIPS] = a[...]
    run = jnp.zeros((HD, HD), F32)
    states[0] = run
    run = line[0, :, :HD]
    states[1] = run
    for i in range(2, X_CHIPS):
        run = line[i - 1, :, :HD] + dot3(line[i - 1, :, HD:], run)
        states[i] = run
    mine = states[x]
    for i in range(Z_CHIPS):
        states[i] = mine if i == 0 else pre[i, :, :HD] + dot3(pre[i, :, HD:], mine)
    for d, o in enumerate((o0, o1, o2, o3)):
        o[...] = states[(z + d) % Z_CHIPS]


def cores_kernel(pos, a0, a1, a2, a3, early, keep_ref, send_ref, line):
    z, first = pos[1], pos[2] == 0
    for d, a in enumerate((a0, a1, a2, a3)):
        line[(z - d + Z_CHIPS) % Z_CHIPS] = a[...]
    for h in range(Z_CHIPS):
        s = line[h]
        t = early[h, :, :HD] + dot3(early[h, :, HD:], s)
        keep_ref[h] = jnp.where(first, s, t)
        send_ref[h] = jnp.where(first, t, s)


def out_kernel(pos, base_ref, map_ref, s_ref, t_ref, gate_ref, gain_ref, o0, o1, o2, o3, rights, *, part):
    per = s_ref.shape[0]
    own = pos[2] == part
    for h in range(per):
        row = wide(jnp.where(own, s_ref[h], t_ref[h]))
        rights[h] = cat([row, row], 0)
    size = o0.shape[0]
    gain = gain_ref[...]
    for d, ref in enumerate((o0, o1, o2, o3)):
        rows = pl.ds(pl.multiple_of((pos[3] + d) % 4 * size, size), size)

        def step(h, _):
            at = (part * per + h) * HD
            cols = pl.ds(pl.multiple_of(at, HD), HD)
            o = base_ref[rows, cols] + fold(mxu(map_ref[rows, pl.ds(pl.multiple_of(2 * at, HD), 2 * HD)], rights[h]))
            g = gate_ref[rows, cols].astype(F32)
            y = o * lax.rsqrt(jnp.mean(o * o, -1, keepdims=True) + 1e-06) * gain * silu(g)
            ref[:, pl.ds(pl.multiple_of(h * HD, HD), HD)] = y.astype(BF16)
            return 0

        lax.fori_loop(0, per, step, 0)


def run_out(pos, base, maps, kept, got, gate, gain, part):
    rows = base.shape[0]
    per = kept.shape[0]
    vmem = pl.BlockSpec(memory_space=pltpu.VMEM)
    return pl.pallas_call(
        functools.partial(out_kernel, part=part),
        in_specs=[pl.BlockSpec(memory_space=pltpu.SMEM)] + [vmem] * 6,
        out_specs=[vmem] * 4,
        out_shape=[jax.ShapeDtypeStruct((rows // 4, per * HD), BF16)] * 4,
        scratch_shapes=[pltpu.VMEM((per, 2 * HD, 2 * HD), BF16)],
        compiler_params=pltpu.CompilerParams(vmem_limit_bytes=LIMIT),
    )(pos, base, maps, kept, got, gate, gain)


def project_kernel(pos, *refs, part, count, offset, extra, final):
    ys, here, there = refs[:count], refs[count : 2 * count], refs[2 * count : 3 * count]
    acc_ref = refs[3 * count] if extra else None
    out_ref, *more = refs[3 * count + extra :]
    depth = ys[0].shape[1]
    tile = 512
    tiles = out_ref.shape[1] // tile

    def sweep(ws):
        for t in range(tiles):
            cols = slice(t * tile, (t + 1) * tile)
            total = acc_ref[:, cols] if extra else None
            for p in range(count):
                term = mxu(ys[p][...], ws[p][offset * p : offset * p + depth, cols])
                total = term if total is None else total + term
            if final:
                more[0][t] = total.astype(BF16)
                store(t).start()
            else:
                out_ref[:, cols] = total

    def store(t):
        return pltpu.make_async_copy(more[0].at[t], out_ref.at[:, pl.ds(t * tile, tile)], more[1].at[t])

    if offset:
        sweep(here)
    else:
        pl.when(pos[2] == part)(lambda: sweep(here))
        pl.when(pos[2] != part)(lambda: sweep(there))
    if final:
        for t in range(tiles):
            store(t).wait()


def project(pos, part, ys, here, there, offset, acc, dtype):
    rows, _ = ys[0].shape
    width = here[0].shape[1]
    count = len(ys)
    final = dtype == BF16
    vmem, hbm = pl.BlockSpec(memory_space=pltpu.VMEM), pl.BlockSpec(memory_space=pl.ANY)
    accs = [] if acc is None else [acc]
    return pl.pallas_call(
        functools.partial(project_kernel, part=part, count=count, offset=offset, extra=len(accs), final=final),
        in_specs=[pl.BlockSpec(memory_space=pltpu.SMEM)] + [vmem] * (3 * count + len(accs)),
        out_specs=hbm if final else vmem,
        out_shape=jax.ShapeDtypeStruct((rows, width), dtype),
        scratch_shapes=[pltpu.VMEM((width // 512, rows, 512), dtype), pltpu.SemaphoreType.DMA((width // 512,))] * final,
        compiler_params=pltpu.CompilerParams(vmem_limit_bytes=LIMIT),
    )(pos, *ys, *here, *there, *accs)


def rim_kernel(q, k, v, out_ref, sem):
    copies, at = [], 0
    for i, ref in enumerate((q, k, v)):
        rows, width = ref.shape
        copies.append(pltpu.make_async_copy(ref.at[pl.ds(rows - 8, 8)], out_ref.at[:, pl.ds(at, width)], sem.at[i]))
        at += width
    for c in copies:
        c.start()
    for c in copies:
        c.wait()


def run_rim(q, k, v):
    hbm = pl.BlockSpec(memory_space=pl.ANY)
    return pl.pallas_call(
        rim_kernel,
        in_specs=[hbm] * 3,
        out_specs=pl.BlockSpec(memory_space=pltpu.VMEM),
        out_shape=jax.ShapeDtypeStruct((8, q.shape[1] + k.shape[1] + v.shape[1]), BF16),
        scratch_shapes=[pltpu.SemaphoreType.DMA((3,))],
        name="rim",
    )(q, k, v)


def half_kernel(pos, w, out_ref, sem):
    rows = out_ref.shape[0]
    start = pl.multiple_of(pos[2] * rows, rows)
    copy = pltpu.make_async_copy(w.at[pl.ds(start, rows)], out_ref, sem)
    copy.start()
    copy.wait()


def run_half(pos, weight, rows):
    return pl.pallas_call(
        half_kernel,
        in_specs=[pl.BlockSpec(memory_space=pltpu.SMEM), pl.BlockSpec(memory_space=pl.ANY)],
        out_specs=pl.BlockSpec(memory_space=pltpu.VMEM),
        out_shape=jax.ShapeDtypeStruct((rows, weight.shape[1]), BF16),
        scratch_shapes=[pltpu.SemaphoreType.DMA(())],
        name="half",
    )(pos, weight)


def ctx_route(dx, dz, dc):
    def dest(i):
        x, z, c = i // (Z_CHIPS * CORES), (i // CORES) % Z_CHIPS, i % CORES
        return ((x + dx) % X_CHIPS * Z_CHIPS + (z + dz) % Z_CHIPS) * CORES + (c + dc) % CORES

    return [(i, dest(i)) for i in range(X_CHIPS * Z_CHIPS * CORES)]


def shards(query_raw, key_raw, value_raw, gate_branch, gate_code, beta_code,
           conv_query, conv_key, conv_value, norm_gain, out_weight):
    ctx = lax.axis_index("ctx")
    head = lax.axis_index("head")
    heads = lax.axis_size("head")
    x, z, core = ctx // (Z_CHIPS * CORES), (ctx // CORES) % Z_CHIPS, ctx % CORES
    pos = jnp.stack([x, z, core, head]).astype(jnp.int32)
    send = lambda a, dx, dz, dc: lax.ppermute(a, "ctx", ctx_route(dx, dz, dc))
    turn = lambda a, d: lax.ppermute(a, "head", [(i, (i + d) % heads) for i in range(heads)])
    hops = (1, 3, 2)
    barrier = lax.optimization_barrier

    n_ctx = lax.axis_size("ctx")
    raws = [pltpu.with_memory_space_constraint(a, pltpu.HBM) for a in (query_raw, key_raw, value_raw)]
    w_rows = out_weight.shape[0] // CORES
    halo = lax.ppermute(run_rim(*raws), "ctx", [(i, i + 1) for i in range(n_ctx - 1)])
    w_mine = run_half(pos, out_weight, w_rows)
    w_got = [turn(w_mine, d) for d in hops]

    base, maps, kept, away = run_scan(pos, *raws, gate_code.T, beta_code.T, halo,
                                      conv_query, conv_key, conv_value)

    line, full = (HD, 2 * HD), (Z_CHIPS, HD, 2 * HD)
    early, *both = vmem_call(pair_kernel, [full] + [line] * 4, [full], pos, kept, send(away, 0, 0, 1))
    lines = [both[0]] + [send(both[d], 0, d, 0) for d in range(1, Z_CHIPS)]
    pre, tot = vmem_call(prefix_kernel, [full, line], [full], pos, *lines)
    tots = [tot] + [send(tot, d, 0, 0) for d in range(1, X_CHIPS)]
    entry = vmem_call(entry_kernel, [(HD, HD)] * 4, [full, (Z_CHIPS, HD, HD)], pos, *tots, pre)
    backs = [entry[0]] + [send(entry[d], 0, d, 0) for d in range(1, Z_CHIPS)]
    own, lent = vmem_call(cores_kernel, [(Z_CHIPS, HD, HD)] * 2, [(Z_CHIPS, HD, HD)], pos, *backs, early)
    got = send(lent, 0, 0, 1)

    gain = norm_gain.reshape(1, HD)
    y_a = run_out(pos, base, maps, own, got, gate_branch, gain, 0)
    a_got = [turn(y_a[d], d) for d in hops]
    _, w_late = barrier((y_a[0], w_got))
    w_other = [send(w, 0, 0, 1) for w in w_late]
    y_b = run_out(pos, base, maps, own, got, gate_branch, gain, 1)
    b_got = [turn(y_b[d], d) for d in hops]
    acc = project(pos, 0, [y_a[0], y_b[0]], [out_weight] * 2, [out_weight] * 2, w_rows, None, F32)
    acc = project(pos, 0, a_got, w_late, w_other, 0, acc, F32)
    return project(pos, 1, b_got, w_late, w_other, 0, acc, BF16)


def solution(mesh):
    return jax.shard_map(
        shards,
        mesh=mesh,
        in_specs=(P("ctx", "head"),) * 6 + (P(None, "head"),) * 3 + (P(), P("head", None)),
        out_specs=P(("ctx", "head"), None),
        check_vma=False,
    )
```

profile of v0, /device:TPU:1, one launch (start us, length us, event | category | flops | bytes accessed | tf_op | source)
XLA Modules:
  0.0 142.4 jit_solution(13814332425236957214)
XLA Ops:
  0.6 3.6 %half.1 = bf16[512,2048]{1,0:T(8,128)(2,1)} custom-call(s32[4]{0:T(128)} %pad_add_fusion.pos, bf16[1024,2048]{1,0:T(8,128)(2,1)} %refs_5_.1), custom_call_target="tpu_custom_call" | custom-call | tf_op jit(solution)/shard_map/half/pallas_call | solution.py:417
  4.3 3.8 %collective-permute-start.17 = (bf16[512,2048]{1,0:T(8,128)(2,1)}, bf16[512,2048]{1,0:T(8,128)(2,1)S(1)}, u32[]{:S(2)}, u32[]{:S(2)}) collective-permute-start(bf16[512,2048]{1,0:T(8,128)(2,1)} %half.1), channel_id=1, source_target_pairs={{0,2},{1,3},{2,0},{3,1},{4,6},{5,7},{6,4},{7,5},{8,10},{9,11},{10,... | collective-permute-start | bytes 6291464 | tf_op jit(solution)/shard_map/ppermute | solution.py:443
  11.0 4.9 %collective-permute-start = (bf16[8,2048]{1,0:T(8,128)(2,1)}, bf16[8,2048]{1,0:T(8,128)(2,1)S(1)}, u32[]{:S(2)}, u32[]{:S(2)}) collective-permute-start(bf16[8,2048]{1,0:T(8,128)(2,1)} %rim.1), channel_id=1, source_target_pairs={{0,4},{4,8},{8,12},{12,16},{16,20},{20,24},{24,28},{28,32},{32,36}... | collective-permute-start | bytes 98312 | tf_op jit(solution)/shard_map/ppermute | solution.py:450
  17.3 39.2 %scan.1 = (f32[1024,1024]{1,0:T(8,128)S(1)}, bf16[1024,2048]{1,0:T(8,128)(2,1)S(1)}, f32[4,128,256]{2,1,0:T(8,128)S(1)}, f32[4,128,256]{2,1,0:T(8,128)S(1)}) custom-call(s32[4]{0:T(128)S(1)} %copy-done.2, bf16[1024,512]{1,0:T(8,128)(2,1)} %q_ref.1, bf16[1024,512]{1,0:T(8,128)(2,1)} %k_ref.1, bf16[1024,1024]{1,0:T(8,128)(2,1)} %v_ref.1, ...), custom_call_target="tpu_custom_call" | custom-call | tf_op jit(solution)/shard_map/scan/pallas_call | solution.py:203
  56.6 1.9 %collective-permute-done.1.got = f32[4,128,256]{2,1,0:T(8,128)S(1)} collective-permute-done((f32[4,128,256]{2,1,0:T(8,128)S(1)}, f32[4,128,256]{2,1,0:T(8,128)S(1)}, u32[]{:S(2)}, u32[]{:S(2)}) %collective-permute-start.1) | collective-permute-done | bytes 524320 | tf_op jit(solution)/shard_map/ppermute | solution.py:442
  59.4 2.0 %collective-permute-start.2 = (f32[128,256]{1,0:T(8,128)S(1)}, f32[128,256]{1,0:T(8,128)S(1)}, u32[]{:S(2)}, u32[]{:S(2)}) collective-permute-start(f32[128,256]{1,0:T(8,128)S(1)} %get-tuple-element.38), channel_id=1, source_target_pairs={{0,8},{4,12},{8,16},{12,20},{16,24},{20,28},{24,0},{28,4},{32,40},... | collective-permute-start | bytes 393224 | tf_op jit(solution)/shard_map/ppermute | solution.py:442
  61.5 3.3 %collective-permute-start.3 = (f32[128,256]{1,0:T(8,128)S(1)}, f32[128,256]{1,0:T(8,128)S(1)}, u32[]{:S(2)}, u32[]{:S(2)}) collective-permute-start(f32[128,256]{1,0:T(8,128)S(1)} %get-tuple-element.39), channel_id=1, source_target_pairs={{0,16},{4,20},{8,24},{12,28},{16,0},{20,4},{24,8},{28,12},{32,48},... | collective-permute-start | bytes 393224 | tf_op jit(solution)/shard_map/ppermute | solution.py:442
  64.8 2.4 %collective-permute-done.2.a1 = f32[128,256]{1,0:T(8,128)S(1)} collective-permute-done((f32[128,256]{1,0:T(8,128)S(1)}, f32[128,256]{1,0:T(8,128)S(1)}, u32[]{:S(2)}, u32[]{:S(2)}) %collective-permute-start.2) | collective-permute-done | bytes 131104 | tf_op jit(solution)/shard_map/ppermute | solution.py:442
  68.4 2.4 %collective-permute-done.3.a2 = f32[128,256]{1,0:T(8,128)S(1)} collective-permute-done((f32[128,256]{1,0:T(8,128)S(1)}, f32[128,256]{1,0:T(8,128)S(1)}, u32[]{:S(2)}, u32[]{:S(2)}) %collective-permute-start.3) | collective-permute-done | bytes 131104 | tf_op jit(solution)/shard_map/ppermute | solution.py:442
  72.6 3.2 %collective-permute-start.7 = (f32[128,256]{1,0:T(8,128)S(1)}, f32[128,256]{1,0:T(8,128)S(1)}, u32[]{:S(2)}, u32[]{:S(2)}) collective-permute-start(f32[128,256]{1,0:T(8,128)S(1)} %get-tuple-element.41.a0), channel_id=1, source_target_pairs={{0,96},{4,100},{8,104},{12,108},{16,112},{20,116},{24,120},{28,124... | collective-permute-start | bytes 393224 | tf_op jit(solution)/shard_map/ppermute | solution.py:442
  76.3 2.2 %collective-permute-done.7.a3 = f32[128,256]{1,0:T(8,128)S(1)} collective-permute-done((f32[128,256]{1,0:T(8,128)S(1)}, f32[128,256]{1,0:T(8,128)S(1)}, u32[]{:S(2)}, u32[]{:S(2)}) %collective-permute-start.7) | collective-permute-done | bytes 131104 | tf_op jit(solution)/shard_map/ppermute | solution.py:442
  78.7 2.4 %collective-permute-done.6.a2 = f32[128,256]{1,0:T(8,128)S(1)} collective-permute-done((f32[128,256]{1,0:T(8,128)S(1)}, f32[128,256]{1,0:T(8,128)S(1)}, u32[]{:S(2)}, u32[]{:S(2)}) %collective-permute-start.6) | collective-permute-done | bytes 131104 | tf_op jit(solution)/shard_map/ppermute | solution.py:442
  81.1 5.1 %collective-permute-done.5.a1 = f32[128,256]{1,0:T(8,128)S(1)} collective-permute-done((f32[128,256]{1,0:T(8,128)S(1)}, f32[128,256]{1,0:T(8,128)S(1)}, u32[]{:S(2)}, u32[]{:S(2)}) %collective-permute-start.5) | collective-permute-done | bytes 131104 | tf_op jit(solution)/shard_map/ppermute | solution.py:442
  87.5 3.0 %collective-permute-start.9 = (f32[128,128]{1,0:T(8,128)S(1)}, f32[128,128]{1,0:T(8,128)S(1)}, u32[]{:S(2)}, u32[]{:S(2)}) collective-permute-start(f32[128,128]{1,0:T(8,128)S(1)} %get-tuple-element.45), channel_id=1, source_target_pairs={{0,16},{4,20},{8,24},{12,28},{16,0},{20,4},{24,8},{28,12},{32,48},... | collective-permute-start | bytes 196616 | tf_op jit(solution)/shard_map/ppermute | solution.py:442
  92.8 2.9 %collective-permute-done.10.a3 = f32[128,128]{1,0:T(8,128)S(1)} collective-permute-done((f32[128,128]{1,0:T(8,128)S(1)}, f32[128,128]{1,0:T(8,128)S(1)}, u32[]{:S(2)}, u32[]{:S(2)}) %collective-permute-start.10) | collective-permute-done | bytes 65568 | tf_op jit(solution)/shard_map/ppermute | solution.py:442
  96.5 4.7 %collective-permute-start.11 = (f32[4,128,128]{2,1,0:T(8,128)S(1)}, f32[4,128,128]{2,1,0:T(8,128)S(1)}, u32[]{:S(2)}, u32[]{:S(2)}) collective-permute-start(f32[4,128,128]{2,1,0:T(8,128)S(1)} %get-tuple-element.49), channel_id=1, source_target_pairs={{0,4},{4,0},{8,12},{12,8},{16,20},{20,16},{24,28},{28,24},{32,36},... | collective-permute-start | bytes 786440 | tf_op jit(solution)/shard_map/ppermute | solution.py:442
  102.4 5.2 %shard_map.114 = (bf16[256,512]{1,0:T(8,128)(2,1)S(1)}, bf16[256,512]{1,0:T(8,128)(2,1)S(1)}, bf16[256,512]{1,0:T(8,128)(2,1)S(1)}, bf16[256,512]{1,0:T(8,128)(2,1)S(1)}) custom-call(s32[4]{0:T(128)S(1)} %copy-done.2, f32[1024,1024]{1,0:T(8,128)S(1)} %get-tuple-element.33.base_ref, bf16[1024,2048]{1,0:T(8,128)(2,1)S(1)} %get-tuple-element.34.map_ref, ...), custom_call_target="tpu_custom_call" | custom-call | tf_op jit(solution)/shard_map/pallas_call | solution.py:323
  108.8 2.4 %collective-permute-start.22 = (bf16[256,512]{1,0:T(8,128)(2,1)S(1)}, bf16[256,512]{1,0:T(8,128)(2,1)S(1)}, u32[]{:S(2)}, u32[]{:S(2)}) collective-permute-start(bf16[256,512]{1,0:T(8,128)(2,1)S(1)} %get-tuple-element.58), channel_id=1, source_target_pairs={{0,3},{1,0},{2,1},{3,2},{4,7},{5,4},{6,5},{7,6},{8,11},{9,8},{10,9... | collective-permute-start | bytes 786440 | tf_op jit(solution)/shard_map/ppermute | solution.py:443
  111.2 6.3 %collective-permute-done.21.refs_0_ = bf16[256,512]{1,0:T(8,128)(2,1)S(1)} collective-permute-done((bf16[256,512]{1,0:T(8,128)(2,1)S(1)}, bf16[256,512]{1,0:T(8,128)(2,1)S(1)}, u32[]{:S(2)}, u32[]{:S(2)}) %collective-permute-start.21) | collective-permute-done | bytes 262176 | tf_op jit(solution)/shard_map/ppermute | solution.py:443
  117.4 5.2 %shard_map.113 = (bf16[256,512]{1,0:T(8,128)(2,1)S(1)}, bf16[256,512]{1,0:T(8,128)(2,1)S(1)}, bf16[256,512]{1,0:T(8,128)(2,1)S(1)}, bf16[256,512]{1,0:T(8,128)(2,1)S(1)}) custom-call(s32[4]{0:T(128)S(1)} %copy-done.2, f32[1024,1024]{1,0:T(8,128)S(1)} %get-tuple-element.33.base_ref, bf16[1024,2048]{1,0:T(8,128)(2,1)S(1)} %get-tuple-element.34.map_ref, ...), custom_call_target="tpu_custom_call" | custom-call | tf_op jit(solution)/shard_map/pallas_call | solution.py:323
  127.1 1.8 %shard_map.115.refs_9_ = f32[256,2048]{1,0:T(8,128)S(1)} custom-call(s32[4]{0:T(128)S(1)} %copy-done.2, bf16[256,512]{1,0:T(8,128)(2,1)S(1)} %get-tuple-element.53.refs_0_, bf16[256,512]{1,0:T(8,128)(2,1)S(1)} %get-tuple-element.60.refs_1_, bf16[1024,2048]{1,0:T(8,128)(2,1)S(1)} %copy-done, bf16[1024,2048]{1,0:T(8,128)(2,1)S(1)} %copy-done, ...), custom_call_target="tpu_custom_call" | custom-call | tf_op jit(solution)/shard_map/pallas_call | solution.py:374
  129.0 4.1 %shard_map.116.refs_9_ = f32[256,2048]{1,0:T(8,128)S(1)} custom-call(s32[4]{0:T(128)S(1)} %copy-done.2, bf16[256,512]{1,0:T(8,128)(2,1)S(1)} %collective-permute-done.21.refs_0_, bf16[256,512]{1,0:T(8,128)(2,1)S(1)} %collective-permute-done.22.refs_1_, bf16[256,512]{1,0:T(8,128)(2,1)S(1)} %collective-permute-done.23.refs_2_, ...), custom_call_target="tpu_custom_call" | custom-call | tf_op jit(solution)/shard_map/pallas_call | solution.py:374
  133.1 4.3 %collective-permute-done.14.refs_2_ = bf16[256,512]{1,0:T(8,128)(2,1)S(1)} collective-permute-done((bf16[256,512]{1,0:T(8,128)(2,1)S(1)}, bf16[256,512]{1,0:T(8,128)(2,1)S(1)}, u32[]{:S(2)}, u32[]{:S(2)}) %collective-permute-start.14) | collective-permute-done | bytes 262176 | tf_op jit(solution)/shard_map/ppermute | solution.py:443
  137.4 4.8 %shard_map.117 = bf16[256,2048]{1,0:T(8,128)(2,1)} custom-call(s32[4]{0:T(128)S(1)} %copy-done.2, bf16[256,512]{1,0:T(8,128)(2,1)S(1)} %collective-permute-done.12.refs_0_, bf16[256,512]{1,0:T(8,128)(2,1)S(1)} %collective-permute-done.13.refs_1_, bf16[256,512]{1,0:T(8,128)(2,1)S(1)} %collective-permute-done.14.refs_2_, ...), custom_call_target="tpu_custom_call" | custom-call | tf_op jit(solution)/shard_map/pallas_call | solution.py:374
  (55 shorter events, 21.0 us)
Async XLA Ops:
  4.3 103.2 %collective-permute-start.17 = (bf16[512,2048]{1,0:T(8,128)(2,1)}, bf16[512,2048]{1,0:T(8,128)(2,1)S(1)}, u32[]{:S(2)}, u32[]{:S(2)}) collective-permute-start(bf16[512,2048]{1,0:T(8,128)(2,1)} %half.1), channel_id=1, source_target_pairs={{0,2},{1,3},{2,0},{3,1},{4,6},{5,7},{6,4},{7,5},{8,10},{9,11},{10,... | collective-permute-start | bytes 6291464 | tf_op jit(solution)/shard_map/ppermute | solution.py:443
  8.1 99.4 %collective-permute-start.16 = (bf16[512,2048]{1,0:T(8,128)(2,1)}, bf16[512,2048]{1,0:T(8,128)(2,1)}, u32[]{:S(2)}, u32[]{:S(2)}) collective-permute-start(bf16[512,2048]{1,0:T(8,128)(2,1)} %half.1), channel_id=1, source_target_pairs={{0,3},{1,0},{2,1},{3,2},{4,7},{5,4},{6,5},{7,6},{8,11},{9,8},{10,9... | collective-permute-start | bytes 6291464 | tf_op jit(solution)/shard_map/ppermute | solution.py:443
  8.9 98.6 %collective-permute-start.15 = (bf16[512,2048]{1,0:T(8,128)(2,1)}, bf16[512,2048]{1,0:T(8,128)(2,1)}, u32[]{:S(2)}, u32[]{:S(2)}) collective-permute-start(bf16[512,2048]{1,0:T(8,128)(2,1)} %half.1), channel_id=1, source_target_pairs={{0,1},{1,2},{2,3},{3,0},{4,5},{5,6},{6,7},{7,4},{8,9},{9,10},{10,1... | collective-permute-start | bytes 6291464 | tf_op jit(solution)/shard_map/ppermute | solution.py:443
  11.0 6.3 %collective-permute-start = (bf16[8,2048]{1,0:T(8,128)(2,1)}, bf16[8,2048]{1,0:T(8,128)(2,1)S(1)}, u32[]{:S(2)}, u32[]{:S(2)}) collective-permute-start(bf16[8,2048]{1,0:T(8,128)(2,1)} %rim.1), channel_id=1, source_target_pairs={{0,4},{4,8},{8,12},{12,16},{16,20},{20,24},{24,28},{28,32},{32,36}... | collective-permute-start | bytes 98312 | tf_op jit(solution)/shard_map/ppermute | solution.py:450
  56.5 2.0 %collective-permute-start.1 = (f32[4,128,256]{2,1,0:T(8,128)S(1)}, f32[4,128,256]{2,1,0:T(8,128)S(1)}, u32[]{:S(2)}, u32[]{:S(2)}) collective-permute-start(f32[4,128,256]{2,1,0:T(8,128)S(1)} %get-tuple-element.36), channel_id=1, source_target_pairs={{0,4},{4,0},{8,12},{12,8},{16,20},{20,16},{24,28},{28,24},{32,36},... | collective-permute-start | bytes 1572872 | tf_op jit(solution)/shard_map/ppermute | solution.py:442
  59.4 7.7 %collective-permute-start.2 = (f32[128,256]{1,0:T(8,128)S(1)}, f32[128,256]{1,0:T(8,128)S(1)}, u32[]{:S(2)}, u32[]{:S(2)}) collective-permute-start(f32[128,256]{1,0:T(8,128)S(1)} %get-tuple-element.38), channel_id=1, source_target_pairs={{0,8},{4,12},{8,16},{12,20},{16,24},{20,28},{24,0},{28,4},{32,40},... | collective-permute-start | bytes 393224 | tf_op jit(solution)/shard_map/ppermute | solution.py:442
  61.5 9.3 %collective-permute-start.3 = (f32[128,256]{1,0:T(8,128)S(1)}, f32[128,256]{1,0:T(8,128)S(1)}, u32[]{:S(2)}, u32[]{:S(2)}) collective-permute-start(f32[128,256]{1,0:T(8,128)S(1)} %get-tuple-element.39), channel_id=1, source_target_pairs={{0,16},{4,20},{8,24},{12,28},{16,0},{20,4},{24,8},{28,12},{32,48},... | collective-permute-start | bytes 393224 | tf_op jit(solution)/shard_map/ppermute | solution.py:442
  67.2 4.3 %collective-permute-start.4 = (f32[128,256]{1,0:T(8,128)S(1)}, f32[128,256]{1,0:T(8,128)S(1)}, u32[]{:S(2)}, u32[]{:S(2)}) collective-permute-start(f32[128,256]{1,0:T(8,128)S(1)} %get-tuple-element.40), channel_id=1, source_target_pairs={{0,24},{4,28},{8,0},{12,4},{16,8},{20,12},{24,16},{28,20},{32,56},... | collective-permute-start | bytes 393224 | tf_op jit(solution)/shard_map/ppermute | solution.py:442
  72.6 5.9 %collective-permute-start.7 = (f32[128,256]{1,0:T(8,128)S(1)}, f32[128,256]{1,0:T(8,128)S(1)}, u32[]{:S(2)}, u32[]{:S(2)}) collective-permute-start(f32[128,256]{1,0:T(8,128)S(1)} %get-tuple-element.41.a0), channel_id=1, source_target_pairs={{0,96},{4,100},{8,104},{12,108},{16,112},{20,116},{24,120},{28,124... | collective-permute-start | bytes 393224 | tf_op jit(solution)/shard_map/ppermute | solution.py:442
  75.8 5.3 %collective-permute-start.6 = (f32[128,256]{1,0:T(8,128)S(1)}, f32[128,256]{1,0:T(8,128)S(1)}, u32[]{:S(2)}, u32[]{:S(2)}) collective-permute-start(f32[128,256]{1,0:T(8,128)S(1)} %get-tuple-element.41.a0), channel_id=1, source_target_pairs={{0,64},{4,68},{8,72},{12,76},{16,80},{20,84},{24,88},{28,92},{32,9... | collective-permute-start | bytes 393224 | tf_op jit(solution)/shard_map/ppermute | solution.py:442
  78.5 7.7 %collective-permute-start.5 = (f32[128,256]{1,0:T(8,128)S(1)}, f32[128,256]{1,0:T(8,128)S(1)}, u32[]{:S(2)}, u32[]{:S(2)}) collective-permute-start(f32[128,256]{1,0:T(8,128)S(1)} %get-tuple-element.41.a0), channel_id=1, source_target_pairs={{0,32},{4,36},{8,40},{12,44},{16,48},{20,52},{24,56},{28,60},{32,6... | collective-permute-start | bytes 393224 | tf_op jit(solution)/shard_map/ppermute | solution.py:442
  87.4 4.8 %collective-permute-start.8 = (f32[128,128]{1,0:T(8,128)S(1)}, f32[128,128]{1,0:T(8,128)S(1)}, u32[]{:S(2)}, u32[]{:S(2)}) collective-permute-start(f32[128,128]{1,0:T(8,128)S(1)} %get-tuple-element.44), channel_id=1, source_target_pairs={{0,8},{4,12},{8,16},{12,20},{16,24},{20,28},{24,0},{28,4},{32,40},... | collective-permute-start | bytes 196616 | tf_op jit(solution)/shard_map/ppermute | solution.py:442
  87.5 5.3 %collective-permute-start.9 = (f32[128,128]{1,0:T(8,128)S(1)}, f32[128,128]{1,0:T(8,128)S(1)}, u32[]{:S(2)}, u32[]{:S(2)}) collective-permute-start(f32[128,128]{1,0:T(8,128)S(1)} %get-tuple-element.45), channel_id=1, source_target_pairs={{0,16},{4,20},{8,24},{12,28},{16,0},{20,4},{24,8},{28,12},{32,48},... | collective-permute-start | bytes 196616 | tf_op jit(solution)/shard_map/ppermute | solution.py:442
  92.2 3.5 %collective-permute-start.10 = (f32[128,128]{1,0:T(8,128)S(1)}, f32[128,128]{1,0:T(8,128)S(1)}, u32[]{:S(2)}, u32[]{:S(2)}) collective-permute-start(f32[128,128]{1,0:T(8,128)S(1)} %get-tuple-element.46), channel_id=1, source_target_pairs={{0,24},{4,28},{8,0},{12,4},{16,8},{20,12},{24,16},{28,20},{32,56},... | collective-permute-start | bytes 196616 | tf_op jit(solution)/shard_map/ppermute | solution.py:442
  96.5 5.8 %collective-permute-start.11 = (f32[4,128,128]{2,1,0:T(8,128)S(1)}, f32[4,128,128]{2,1,0:T(8,128)S(1)}, u32[]{:S(2)}, u32[]{:S(2)}) collective-permute-start(f32[4,128,128]{2,1,0:T(8,128)S(1)} %get-tuple-element.49), channel_id=1, source_target_pairs={{0,4},{4,0},{8,12},{12,8},{16,20},{20,16},{24,28},{28,24},{32,36},... | collective-permute-start | bytes 786440 | tf_op jit(solution)/shard_map/ppermute | solution.py:442
  107.5 19.1 %collective-permute-start.18 = (bf16[512,2048]{1,0:T(8,128)(2,1)}, bf16[512,2048]{1,0:T(8,128)(2,1)S(1)}, u32[]{:S(2)}, u32[]{:S(2)}) collective-permute-start(bf16[512,2048]{1,0:T(8,128)(2,1)} %collective-permute-done.15.refs_3_), channel_id=1, source_target_pairs={{0,4},{4,0},{8,12},{12,8},{16,20},{20,16},{24,28},{28,24},{32,36},... | collective-permute-start | bytes 6291464 | tf_op jit(solution)/shard_map/ppermute | solution.py:442
  108.0 21.0 %collective-permute-start.19 = (bf16[512,2048]{1,0:T(8,128)(2,1)}, bf16[512,2048]{1,0:T(8,128)(2,1)S(1)}, u32[]{:S(2)}, u32[]{:S(2)}) collective-permute-start(bf16[512,2048]{1,0:T(8,128)(2,1)} %collective-permute-done.16.refs_4_), channel_id=1, source_target_pairs={{0,4},{4,0},{8,12},{12,8},{16,20},{20,16},{24,28},{28,24},{32,36},... | collective-permute-start | bytes 6291464 | tf_op jit(solution)/shard_map/ppermute | solution.py:442
  108.1 20.8 %collective-permute-start.20 = (bf16[512,2048]{1,0:T(8,128)(2,1)S(1)}, bf16[512,2048]{1,0:T(8,128)(2,1)S(1)}, u32[]{:S(2)}, u32[]{:S(2)}) collective-permute-start(bf16[512,2048]{1,0:T(8,128)(2,1)S(1)} %collective-permute-done.17.refs_5_), channel_id=1, source_target_pairs={{0,4},{4,0},{8,12},{12,8},{16,20},{20,16},{24,28},{28,24},{32,36},... | collective-permute-start | bytes 6291464 | tf_op jit(solution)/shard_map/ppermute | solution.py:442
  108.5 8.9 %collective-permute-start.21 = (bf16[256,512]{1,0:T(8,128)(2,1)S(1)}, bf16[256,512]{1,0:T(8,128)(2,1)S(1)}, u32[]{:S(2)}, u32[]{:S(2)}) collective-permute-start(bf16[256,512]{1,0:T(8,128)(2,1)S(1)} %get-tuple-element.57), channel_id=1, source_target_pairs={{0,1},{1,2},{2,3},{3,0},{4,5},{5,6},{6,7},{7,4},{8,9},{9,10},{10,1... | collective-permute-start | bytes 786440 | tf_op jit(solution)/shard_map/ppermute | solution.py:443
  108.8 13.8 %collective-permute-start.22 = (bf16[256,512]{1,0:T(8,128)(2,1)S(1)}, bf16[256,512]{1,0:T(8,128)(2,1)S(1)}, u32[]{:S(2)}, u32[]{:S(2)}) collective-permute-start(bf16[256,512]{1,0:T(8,128)(2,1)S(1)} %get-tuple-element.58), channel_id=1, source_target_pairs={{0,3},{1,0},{2,1},{3,2},{4,7},{5,4},{6,5},{7,6},{8,11},{9,8},{10,9... | collective-permute-start | bytes 786440 | tf_op jit(solution)/shard_map/ppermute | solution.py:443
  117.4 8.4 %collective-permute-start.23 = (bf16[256,512]{1,0:T(8,128)(2,1)S(1)}, bf16[256,512]{1,0:T(8,128)(2,1)S(1)}, u32[]{:S(2)}, u32[]{:S(2)}) collective-permute-start(bf16[256,512]{1,0:T(8,128)(2,1)S(1)} %get-tuple-element.59), channel_id=1, source_target_pairs={{0,2},{1,3},{2,0},{3,1},{4,6},{5,7},{6,4},{7,5},{8,10},{9,11},{10,... | collective-permute-start | bytes 786440 | tf_op jit(solution)/shard_map/ppermute | solution.py:443
  122.6 10.4 %collective-permute-start.12 = (bf16[256,512]{1,0:T(8,128)(2,1)S(1)}, bf16[256,512]{1,0:T(8,128)(2,1)S(1)}, u32[]{:S(2)}, u32[]{:S(2)}) collective-permute-start(bf16[256,512]{1,0:T(8,128)(2,1)S(1)} %get-tuple-element.50), channel_id=1, source_target_pairs={{0,1},{1,2},{2,3},{3,0},{4,5},{5,6},{6,7},{7,4},{8,9},{9,10},{10,1... | collective-permute-start | bytes 786440 | tf_op jit(solution)/shard_map/ppermute | solution.py:443
  125.8 7.2 %collective-permute-start.13 = (bf16[256,512]{1,0:T(8,128)(2,1)S(1)}, bf16[256,512]{1,0:T(8,128)(2,1)S(1)}, u32[]{:S(2)}, u32[]{:S(2)}) collective-permute-start(bf16[256,512]{1,0:T(8,128)(2,1)S(1)} %get-tuple-element.51), channel_id=1, source_target_pairs={{0,3},{1,0},{2,1},{3,2},{4,7},{5,4},{6,5},{7,6},{8,11},{9,8},{10,9... | collective-permute-start | bytes 786440 | tf_op jit(solution)/shard_map/ppermute | solution.py:443
  126.6 10.8 %collective-permute-start.14 = (bf16[256,512]{1,0:T(8,128)(2,1)S(1)}, bf16[256,512]{1,0:T(8,128)(2,1)S(1)}, u32[]{:S(2)}, u32[]{:S(2)}) collective-permute-start(bf16[256,512]{1,0:T(8,128)(2,1)S(1)} %get-tuple-element.52), channel_id=1, source_target_pairs={{0,2},{1,3},{2,0},{3,1},{4,6},{5,7},{6,4},{7,5},{8,10},{9,11},{10,... | collective-permute-start | bytes 786440 | tf_op jit(solution)/shard_map/ppermute | solution.py:443
  (9 other events, 179.5 us)
where the time goes:
time: 144 us; the launch traced here: 142 us
  Pallas kernels  69.2 us (48%)
  waiting for transfers between devices  36.6 us (25%)
  starting transfers between devices  35.5 us (25%)
    pallas_call x1, Pallas kernels, run_scan(): pl.pallas_call(scan_kernel, grid=(rows // BLOCK,), in_specs=[pl.BlockSpec...  39.2 us
    ppermute x14, waiting for transfers between devices, shards(): send = lambda a, dx, dz, dc: lax.ppermute(a, 'ctx', ctx_route(dx, dz, dc))  22.9 us
    ppermute x14, starting transfers between devices, shards(): send = lambda a, dx, dz, dc: lax.ppermute(a, 'ctx', ctx_route(dx, dz, dc))  19.9 us
    ppermute x9, waiting for transfers between devices, shards(): lax.ppermute(a, 'head', [(i, (i + d) % heads) for i in range(heads)])  12.4 us
    pallas_call x3, Pallas kernels, project(): pl.pallas_call(functools.partial(project_kernel, part=part, count=count,...  10.7 us
    ppermute x9, starting transfers between devices, shards(): lax.ppermute(a, 'head', [(i, (i + d) % heads) for i in range(heads)])  10.7 us
    pallas_call x2, Pallas kernels, run_out(): pl.pallas_call(functools.partial(out_kernel, part=part), in_specs=[pl.Blo...  10.3 us
    ppermute x1, starting transfers between devices, shards(): lax.ppermute(run_rim(*raws), 'ctx', [(i, i + 1) for i in range(n_ctx - 1)])  4.95 us
  transfers between devices with their start and end apart: 24, of which 14 were waited for; matrix products, arithmetic and copies ran while one was open for 0% of the time, Pallas kernels for 43%

commit v1 on v0

--- a/solution.py
+++ b/solution.py
@@ -13,7 +13,7 @@
 HD = 128
 BLOCK = 64
 KERNEL = 4
-LIMIT = 12 << 20
+LIMIT = 6 << 20
 
 
 def split(x):
@@ -210,7 +210,7 @@
         + [jax.ShapeDtypeStruct(half, F32)] * 2,
         scratch_shapes=[pltpu.VMEM((vh, HD, 2 * HD), F32), pltpu.VMEM((8, 2 * kw + vw), F32),
                         pltpu.VMEM((2, rows, vh), F32)],
-        compiler_params=pltpu.CompilerParams(dimension_semantics=("arbitrary",), vmem_limit_bytes=20 << 20),
+        compiler_params=pltpu.CompilerParams(dimension_semantics=("arbitrary",), vmem_limit_bytes=10 << 20),
         name="scan",
     )(pos, q, k, v, gc, bc, halo, cq, ck, cv)
 
@@ -330,10 +330,11 @@
     )(pos, base, maps, kept, got, gate, gain)
 
 
-def project_kernel(pos, *refs, part, count, offset, extra, final):
-    ys, here, there = refs[:count], refs[count : 2 * count], refs[2 * count : 3 * count]
-    acc_ref = refs[3 * count] if extra else None
-    out_ref, *more = refs[3 * count + extra :]
+def project_kernel(pos, *refs, starts, picks, held, count, extra, final):
+    ys, ws = refs[:count], refs[count : count + held]
+    here, there = [ws[i] for i in picks[0]], [ws[i] for i in picks[1]]
+    acc_ref = refs[count + held] if extra else None
+    out_ref, *more = refs[count + held + extra :]
     depth = ys[0].shape[1]
     tile = 512
     tiles = out_ref.shape[1] // tile
@@ -343,7 +344,7 @@
             cols = slice(t * tile, (t + 1) * tile)
             total = acc_ref[:, cols] if extra else None
             for p in range(count):
-                term = mxu(ys[p][...], ws[p][offset * p : offset * p + depth, cols])
+                term = mxu(ys[p][...], ws[p][starts[p] : starts[p] + depth, cols])
                 total = term if total is None else total + term
             if final:
                 more[0][t] = total.astype(BF16)
@@ -354,31 +355,57 @@
     def store(t):
         return pltpu.make_async_copy(more[0].at[t], out_ref.at[:, pl.ds(t * tile, tile)], more[1].at[t])
 
-    if offset:
+    if picks[0] == picks[1]:
         sweep(here)
     else:
-        pl.when(pos[2] == part)(lambda: sweep(here))
-        pl.when(pos[2] != part)(lambda: sweep(there))
+        pl.when(pos[2] == 0)(lambda: sweep(here))
+        pl.when(pos[2] != 0)(lambda: sweep(there))
     if final:
         for t in range(tiles):
             store(t).wait()
 
 
-def project(pos, part, ys, here, there, offset, acc, dtype):
+def project(pos, starts, ys, weights, picks, acc, dtype):
     rows, _ = ys[0].shape
-    width = here[0].shape[1]
+    width = weights[0].shape[1]
     count = len(ys)
     final = dtype == BF16
     vmem, hbm = pl.BlockSpec(memory_space=pltpu.VMEM), pl.BlockSpec(memory_space=pl.ANY)
     accs = [] if acc is None else [acc]
     return pl.pallas_call(
-        functools.partial(project_kernel, part=part, count=count, offset=offset, extra=len(accs), final=final),
-        in_specs=[pl.BlockSpec(memory_space=pltpu.SMEM)] + [vmem] * (3 * count + len(accs)),
+        functools.partial(project_kernel, starts=starts, picks=picks, held=len(weights), count=count, extra=len(accs), final=final),
+        in_specs=[pl.BlockSpec(memory_space=pltpu.SMEM)] + [vmem] * (count + len(weights) + len(accs)),
         out_specs=hbm if final else vmem,
         out_shape=jax.ShapeDtypeStruct((rows, width), dtype),
         scratch_shapes=[pltpu.VMEM((width // 512, rows, 512), dtype), pltpu.SemaphoreType.DMA((width // 512,))] * final,
+        compiler_params=pltpu.CompilerParams(vmem_limit_bytes=14 << 20),
+    )(pos, *ys, *weights, *accs)
+
+
+def fetch_kernel(*refs):
+    sem = refs[-1]
+    copies = []
+    for i in range(2):
+        rows = refs[i].shape[0] // 4
+        for j in range(4):
+            part = pl.ds(j * rows, rows)
+            copies.append(pltpu.make_async_copy(refs[i].at[part], refs[2 + i].at[part], sem.at[i, j]))
+    for c in copies:
+        c.start()
+    for c in copies:
+        c.wait()
+
+
+def run_fetch(*arrays):
+    return pl.pallas_call(
+        fetch_kernel,
+        in_specs=[pl.BlockSpec(memory_space=pl.ANY)] * 2,
+        out_specs=[pl.BlockSpec(memory_space=pltpu.VMEM)] * 2,
+        out_shape=[jax.ShapeDtypeStruct(a.shape, a.dtype) for a in arrays],
+        scratch_shapes=[pltpu.SemaphoreType.DMA((2, 4))],
         compiler_params=pltpu.CompilerParams(vmem_limit_bytes=LIMIT),
-    )(pos, *ys, *here, *there, *accs)
+        name="fetch",
+    )(*arrays)
 
 
 def rim_kernel(q, k, v, out_ref, sem):
@@ -405,31 +432,19 @@
     )(q, k, v)
 
 
-def half_kernel(pos, w, out_ref, sem):
-    rows = out_ref.shape[0]
-    start = pl.multiple_of(pos[2] * rows, rows)
-    copy = pltpu.make_async_copy(w.at[pl.ds(start, rows)], out_ref, sem)
-    copy.start()
-    copy.wait()
-
-
-def run_half(pos, weight, rows):
-    return pl.pallas_call(
-        half_kernel,
-        in_specs=[pl.BlockSpec(memory_space=pltpu.SMEM), pl.BlockSpec(memory_space=pl.ANY)],
-        out_specs=pl.BlockSpec(memory_space=pltpu.VMEM),
-        out_shape=jax.ShapeDtypeStruct((rows, weight.shape[1]), BF16),
-        scratch_shapes=[pltpu.SemaphoreType.DMA(())],
-        name="half",
-    )(pos, weight)
-
-
 def ctx_route(dx, dz, dc):
     def dest(i):
         x, z, c = i // (Z_CHIPS * CORES), (i // CORES) % Z_CHIPS, i % CORES
         return ((x + dx) % X_CHIPS * Z_CHIPS + (z + dz) % Z_CHIPS) * CORES + (c + dc) % CORES
 
     return [(i, dest(i)) for i in range(X_CHIPS * Z_CHIPS * CORES)]
+
+
+def mesh_route(n_ctx, heads, moves):
+    row = Z_CHIPS * CORES
+    pairs = [(c, h) for c in range(n_ctx) for h in range(heads)]
+    dest = lambda c, h, dx, dy: (c + dx * row) % n_ctx * heads + (h + dy) % heads
+    return [(c * heads + h, dest(c, h, *moves[c % CORES])) for c, h in pairs]
 
 
 def shards(query_raw, key_raw, value_raw, gate_branch, gate_code, beta_code,
@@ -448,8 +463,8 @@
     raws = [pltpu.with_memory_space_constraint(a, pltpu.HBM) for a in (query_raw, key_raw, value_raw)]
     w_rows = out_weight.shape[0] // CORES
     halo = lax.ppermute(run_rim(*raws), "ctx", [(i, i + 1) for i in range(n_ctx - 1)])
-    w_mine = run_half(pos, out_weight, w_rows)
-    w_got = [turn(w_mine, d) for d in hops]
+    w_first = lax.ppermute(out_weight, ("ctx", "head"), mesh_route(n_ctx, heads, ((0, 2), (0, 1))))
+    w_second = lax.ppermute(out_weight, ("ctx", "head"), mesh_route(n_ctx, heads, ((1, 0), (0, 3))))
 
     base, maps, kept, away = run_scan(pos, *raws, gate_code.T, beta_code.T, halo,
                                       conv_query, conv_key, conv_value)
@@ -467,13 +482,16 @@
     gain = norm_gain.reshape(1, HD)
     y_a = run_out(pos, base, maps, own, got, gate_branch, gain, 0)
     a_got = [turn(y_a[d], d) for d in hops]
-    _, w_late = barrier((y_a[0], w_got))
-    w_other = [send(w, 0, 0, 1) for w in w_late]
     y_b = run_out(pos, base, maps, own, got, gate_branch, gain, 1)
     b_got = [turn(y_b[d], d) for d in hops]
-    acc = project(pos, 0, [y_a[0], y_b[0]], [out_weight] * 2, [out_weight] * 2, w_rows, None, F32)
-    acc = project(pos, 0, a_got, w_late, w_other, 0, acc, F32)
-    return project(pos, 1, b_got, w_late, w_other, 0, acc, BF16)
+    _, w_first, w_second = barrier((y_b[0], w_first, w_second))
+    swap_first, swap_second = send(w_first, 0, 0, 1), send(w_second, 0, 0, 1)
+    acc = project(pos, (0, w_rows), [y_a[0], y_b[0]], [out_weight], ((0, 0),) * 2, None, F32)
+    acc, w_first, w_second = barrier((acc, w_first, w_second))
+    held = [*run_fetch(w_first, w_second), swap_first, swap_second]
+    picks = ((2, 3, 0), (0, 1, 2))
+    acc = project(pos, (0,) * 3, a_got, held, picks, acc, F32)
+    return project(pos, (w_rows,) * 3, b_got, held, picks, acc, BF16)
 
 
 def solution(mesh):

time: 144 us -> 132 us (0.917)
  the two profiles are of different devices: /device:TPU:1 before, /device:TPU:0 now
where the time goes in v1:
time: 132 us
  Pallas kernels  65.6 us (50%)
  starting transfers between devices  35.8 us (27%)
  waiting for transfers between devices  30.1 us (23%)
    pallas_call x1, Pallas kernels, run_scan(): pl.pallas_call(scan_kernel, grid=(rows // BLOCK,), in_specs=[pl.BlockSpec...  39.2 us
    ppermute x13, starting transfers between devices, shards(): send = lambda a, dx, dz, dc: lax.ppermute(a, 'ctx', ctx_route(dx, dz, dc))  22 us
    ppermute x13, waiting for transfers between devices, shards(): send = lambda a, dx, dz, dc: lax.ppermute(a, 'ctx', ctx_route(dx, dz, dc))  15.9 us
    ppermute x6, waiting for transfers between devices, shards(): lax.ppermute(a, 'head', [(i, (i + d) % heads) for i in range(heads)])  12.6 us
    pallas_call x2, Pallas kernels, run_out(): pl.pallas_call(functools.partial(out_kernel, part=part), in_specs=[pl.Blo...  10.3 us
    ppermute x6, starting transfers between devices, shards(): lax.ppermute(a, 'head', [(i, (i + d) % heads) for i in range(heads)])  7.46 us
    pallas_call x3, Pallas kernels, project(): pl.pallas_call(functools.partial(project_kernel, starts=starts, picks=pic...  7.2 us
    pallas_call x4, Pallas kernels, vmem_call(): pl.pallas_call(body, in_specs=[pl.BlockSpec(memory_space=pltpu.SMEM)] + [...  4.03 us
  transfers between devices with their start and end apart: 22, of which 13 were waited for; matrix products, arithmetic and copies ran while one was open for 0% of the time, Pallas kernels for 47%

profile of v1, /device:TPU:0, one launch (start us, length us, event | category | flops | bytes accessed | tf_op | source)
XLA Modules:
  0.0 131.9 jit_solution(4610210571593132877)
XLA Ops:
  0.0 3.4 %collective-permute-start.15 = (bf16[1024,2048]{1,0:T(8,128)(2,1)}, bf16[1024,2048]{1,0:T(8,128)(2,1)}, u32[]{:S(2)}, u32[]{:S(2)}) collective-permute-start(bf16[1024,2048]{1,0:T(8,128)(2,1)} %refs_2_.1), channel_id=1, source_target_pairs={{0,2},{1,3},{2,0},{3,1},{4,5},{5,6},{6,7},{7,4},{8,10},{9,11},{10,... | collective-permute-start | bytes 12582920 | tf_op jit(solution)/shard_map/ppermute | solution.py:466
  3.4 1.5 %collective-permute-start.16 = (bf16[1024,2048]{1,0:T(8,128)(2,1)}, bf16[1024,2048]{1,0:T(8,128)(2,1)}, u32[]{:S(2)}, u32[]{:S(2)}) collective-permute-start(bf16[1024,2048]{1,0:T(8,128)(2,1)} %refs_2_.1), channel_id=1, source_target_pairs={{0,32},{1,33},{2,34},{3,35},{4,7},{5,4},{6,5},{7,6},{8,40},{9,41},... | collective-permute-start | bytes 12582920 | tf_op jit(solution)/shard_map/ppermute | solution.py:467
  8.8 39.2 %scan.1 = (f32[1024,1024]{1,0:T(8,128)S(1)}, bf16[1024,2048]{1,0:T(8,128)(2,1)S(1)}, f32[4,128,256]{2,1,0:T(8,128)S(1)}, f32[4,128,256]{2,1,0:T(8,128)S(1)}) custom-call(s32[4]{0:T(128)S(1)} %pad_add_fusion.pos, bf16[1024,512]{1,0:T(8,128)(2,1)} %q_ref.1, bf16[1024,512]{1,0:T(8,128)(2,1)} %k_ref.1, bf16[1024,1024]{1,0:T(8,128)(2,1)} %v_ref.1, ...), custom_call_target="tpu_custom_call" | custom-call | tf_op jit(solution)/shard_map/scan/pallas_call | solution.py:203
  48.0 3.0 %collective-permute-start.1 = (f32[4,128,256]{2,1,0:T(8,128)S(1)}, f32[4,128,256]{2,1,0:T(8,128)S(1)}, u32[]{:S(2)}, u32[]{:S(2)}) collective-permute-start(f32[4,128,256]{2,1,0:T(8,128)S(1)} %get-tuple-element.40), channel_id=1, source_target_pairs={{0,4},{4,0},{8,12},{12,8},{16,20},{20,16},{24,28},{28,24},{32,36},... | collective-permute-start | bytes 1572872 | tf_op jit(solution)/shard_map/ppermute | solution.py:457
  51.0 1.5 %collective-permute-done.1.got = f32[4,128,256]{2,1,0:T(8,128)S(1)} collective-permute-done((f32[4,128,256]{2,1,0:T(8,128)S(1)}, f32[4,128,256]{2,1,0:T(8,128)S(1)}, u32[]{:S(2)}, u32[]{:S(2)}) %collective-permute-start.1) | collective-permute-done | bytes 524320 | tf_op jit(solution)/shard_map/ppermute | solution.py:457
  53.5 2.5 %collective-permute-start.2 = (f32[128,256]{1,0:T(8,128)S(1)}, f32[128,256]{1,0:T(8,128)S(1)}, u32[]{:S(2)}, u32[]{:S(2)}) collective-permute-start(f32[128,256]{1,0:T(8,128)S(1)} %get-tuple-element.42), channel_id=1, source_target_pairs={{0,8},{4,12},{8,16},{12,20},{16,24},{20,28},{24,0},{28,4},{32,40},... | collective-permute-start | bytes 393224 | tf_op jit(solution)/shard_map/ppermute | solution.py:457
  56.0 3.6 %collective-permute-start.3 = (f32[128,256]{1,0:T(8,128)S(1)}, f32[128,256]{1,0:T(8,128)S(1)}, u32[]{:S(2)}, u32[]{:S(2)}) collective-permute-start(f32[128,256]{1,0:T(8,128)S(1)} %get-tuple-element.43), channel_id=1, source_target_pairs={{0,16},{4,20},{8,24},{12,28},{16,0},{20,4},{24,8},{28,12},{32,48},... | collective-permute-start | bytes 393224 | tf_op jit(solution)/shard_map/ppermute | solution.py:457
  61.9 4.0 %collective-permute-done.3.a2 = f32[128,256]{1,0:T(8,128)S(1)} collective-permute-done((f32[128,256]{1,0:T(8,128)S(1)}, f32[128,256]{1,0:T(8,128)S(1)}, u32[]{:S(2)}, u32[]{:S(2)}) %collective-permute-start.3) | collective-permute-done | bytes 131104 | tf_op jit(solution)/shard_map/ppermute | solution.py:457
  67.0 2.3 %collective-permute-start.5 = (f32[128,256]{1,0:T(8,128)S(1)}, f32[128,256]{1,0:T(8,128)S(1)}, u32[]{:S(2)}, u32[]{:S(2)}) collective-permute-start(f32[128,256]{1,0:T(8,128)S(1)} %get-tuple-element.45.a0), channel_id=1, source_target_pairs={{0,32},{4,36},{8,40},{12,44},{16,48},{20,52},{24,56},{28,60},{32,6... | collective-permute-start | bytes 393224 | tf_op jit(solution)/shard_map/ppermute | solution.py:457
  69.3 1.7 %collective-permute-start.6 = (f32[128,256]{1,0:T(8,128)S(1)}, f32[128,256]{1,0:T(8,128)S(1)}, u32[]{:S(2)}, u32[]{:S(2)}) collective-permute-start(f32[128,256]{1,0:T(8,128)S(1)} %get-tuple-element.45.a0), channel_id=1, source_target_pairs={{0,64},{4,68},{8,72},{12,76},{16,80},{20,84},{24,88},{28,92},{32,9... | collective-permute-start | bytes 393224 | tf_op jit(solution)/shard_map/ppermute | solution.py:457
  71.1 2.2 %collective-permute-start.7 = (f32[128,256]{1,0:T(8,128)S(1)}, f32[128,256]{1,0:T(8,128)S(1)}, u32[]{:S(2)}, u32[]{:S(2)}) collective-permute-start(f32[128,256]{1,0:T(8,128)S(1)} %get-tuple-element.45.a0), channel_id=1, source_target_pairs={{0,96},{4,100},{8,104},{12,108},{16,112},{20,116},{24,120},{28,124... | collective-permute-start | bytes 393224 | tf_op jit(solution)/shard_map/ppermute | solution.py:457
  74.6 1.9 %collective-permute-done.6.a2 = f32[128,256]{1,0:T(8,128)S(1)} collective-permute-done((f32[128,256]{1,0:T(8,128)S(1)}, f32[128,256]{1,0:T(8,128)S(1)}, u32[]{:S(2)}, u32[]{:S(2)}) %collective-permute-start.6) | collective-permute-done | bytes 131104 | tf_op jit(solution)/shard_map/ppermute | solution.py:457
  77.7 1.7 %collective-permute-start.8 = (f32[128,128]{1,0:T(8,128)S(1)}, f32[128,128]{1,0:T(8,128)S(1)}, u32[]{:S(2)}, u32[]{:S(2)}) collective-permute-start(f32[128,128]{1,0:T(8,128)S(1)} %get-tuple-element.48), channel_id=1, source_target_pairs={{0,8},{4,12},{8,16},{12,20},{16,24},{20,28},{24,0},{28,4},{32,40},... | collective-permute-start | bytes 196616 | tf_op jit(solution)/shard_map/ppermute | solution.py:457
  79.3 3.4 %collective-permute-start.9 = (f32[128,128]{1,0:T(8,128)S(1)}, f32[128,128]{1,0:T(8,128)S(1)}, u32[]{:S(2)}, u32[]{:S(2)}) collective-permute-start(f32[128,128]{1,0:T(8,128)S(1)} %get-tuple-element.49), channel_id=1, source_target_pairs={{0,16},{4,20},{8,24},{12,28},{16,0},{20,4},{24,8},{28,12},{32,48},... | collective-permute-start | bytes 196616 | tf_op jit(solution)/shard_map/ppermute | solution.py:457
  87.9 1.5 %collective-permute-done.11.t_ref = f32[4,128,128]{2,1,0:T(8,128)S(1)} collective-permute-done((f32[4,128,128]{2,1,0:T(8,128)S(1)}, f32[4,128,128]{2,1,0:T(8,128)S(1)}, u32[]{:S(2)}, u32[]{:S(2)}) %collective-permute-start.11) | collective-permute-done | bytes 262176 | tf_op jit(solution)/shard_map/ppermute | solution.py:457
  89.5 5.1 %shard_map.113 = (bf16[256,512]{1,0:T(8,128)(2,1)S(1)}, bf16[256,512]{1,0:T(8,128)(2,1)S(1)}, bf16[256,512]{1,0:T(8,128)(2,1)S(1)}, bf16[256,512]{1,0:T(8,128)(2,1)S(1)}) custom-call(s32[4]{0:T(128)S(1)} %pad_add_fusion.pos, f32[1024,1024]{1,0:T(8,128)S(1)} %get-tuple-element.37.base_ref, bf16[1024,2048]{1,0:T(8,128)(2,1)S(1)} %get-tuple-element.38.map_ref, ...), custom_call_target="tpu_custom_call" | custom-call | tf_op jit(solution)/shard_map/pallas_call | solution.py:323
  95.8 5.2 %shard_map.114 = (bf16[256,512]{1,0:T(8,128)(2,1)S(1)}, bf16[256,512]{1,0:T(8,128)(2,1)S(1)}, bf16[256,512]{1,0:T(8,128)(2,1)S(1)}, bf16[256,512]{1,0:T(8,128)(2,1)S(1)}) custom-call(s32[4]{0:T(128)S(1)} %pad_add_fusion.pos, f32[1024,1024]{1,0:T(8,128)S(1)} %get-tuple-element.37.base_ref, bf16[1024,2048]{1,0:T(8,128)(2,1)S(1)} %get-tuple-element.38.map_ref, ...), custom_call_target="tpu_custom_call" | custom-call | tf_op jit(solution)/shard_map/pallas_call | solution.py:323
  102.2 2.1 %collective-permute-start.20 = (bf16[256,512]{1,0:T(8,128)(2,1)S(1)}, bf16[256,512]{1,0:T(8,128)(2,1)S(1)}, u32[]{:S(2)}, u32[]{:S(2)}) collective-permute-start(bf16[256,512]{1,0:T(8,128)(2,1)S(1)} %get-tuple-element.66), channel_id=1, source_target_pairs={{0,3},{1,0},{2,1},{3,2},{4,7},{5,4},{6,5},{7,6},{8,11},{9,8},{10,9... | collective-permute-start | bytes 786440 | tf_op jit(solution)/shard_map/ppermute | solution.py:458
  104.3 11.2 %collective-permute-done.19.refs_0_ = bf16[256,512]{1,0:T(8,128)(2,1)S(1)} collective-permute-done((bf16[256,512]{1,0:T(8,128)(2,1)S(1)}, bf16[256,512]{1,0:T(8,128)(2,1)S(1)}, u32[]{:S(2)}, u32[]{:S(2)}) %collective-permute-start.19) | collective-permute-done | bytes 262176 | tf_op jit(solution)/shard_map/ppermute | solution.py:458
  115.5 4.1 %collective-permute-start.13 = (bf16[256,512]{1,0:T(8,128)(2,1)S(1)}, bf16[256,512]{1,0:T(8,128)(2,1)S(1)}, u32[]{:S(2)}, u32[]{:S(2)}) collective-permute-start(bf16[256,512]{1,0:T(8,128)(2,1)S(1)} %get-tuple-element.55), channel_id=1, source_target_pairs={{0,3},{1,0},{2,1},{3,2},{4,7},{5,4},{6,5},{7,6},{8,11},{9,8},{10,9... | collective-permute-start | bytes 786440 | tf_op jit(solution)/shard_map/ppermute | solution.py:458
  119.6 1.8 %shard_map.115.refs_7_ = f32[256,2048]{1,0:T(8,128)S(1)} custom-call(s32[4]{0:T(128)S(1)} %pad_add_fusion.pos, bf16[256,512]{1,0:T(8,128)(2,1)S(1)} %get-tuple-element.57.refs_0_, bf16[256,512]{1,0:T(8,128)(2,1)S(1)} %get-tuple-element.58.refs_1_, bf16[1024,2048]{1,0:T(8,128)(2,1)S(1)} %copy-done.1), custom_call_target="tpu_custom_call" | custom-call | tf_op jit(solution)/shard_map/pallas_call | solution.py:375
  121.4 3.5 %fetch.1 = (bf16[1024,2048]{1,0:T(8,128)(2,1)S(1)}, bf16[1024,2048]{1,0:T(8,128)(2,1)S(1)}) custom-call(bf16[1024,2048]{1,0:T(8,128)(2,1)} %collective-permute-done.15.refs_0_, bf16[1024,2048]{1,0:T(8,128)(2,1)} %collective-permute-done.16.refs_1_), custom_call_target="tpu_custom_call" | custom-call | tf_op jit(solution)/shard_map/fetch/pallas_call | solution.py:400
  124.9 2.3 %shard_map.116.refs_7_ = f32[256,2048]{1,0:T(8,128)S(1)} custom-call(s32[4]{0:T(128)S(1)} %pad_add_fusion.pos, bf16[256,512]{1,0:T(8,128)(2,1)S(1)} %collective-permute-done.19.refs_0_, bf16[256,512]{1,0:T(8,128)(2,1)S(1)} %collective-permute-done.20.refs_1_, bf16[256,512]{1,0:T(8,128)(2,1)S(1)} %collective-permute-done.21.refs_2_, ...), custom_call_target="tpu_custom_call" | custom-call | tf_op jit(solution)/shard_map/pallas_call | solution.py:375
  128.7 3.1 %shard_map.117 = bf16[256,2048]{1,0:T(8,128)(2,1)} custom-call(s32[4]{0:T(128)S(1)} %pad_add_fusion.pos, bf16[256,512]{1,0:T(8,128)(2,1)S(1)} %collective-permute-done.12.refs_0_, bf16[256,512]{1,0:T(8,128)(2,1)S(1)} %collective-permute-done.13.refs_1_, bf16[256,512]{1,0:T(8,128)(2,1)S(1)} %collective-permute-done.14.refs_2_, ...), custom_call_target="tpu_custom_call" | custom-call | tf_op jit(solution)/shard_map/pallas_call | solution.py:375
  (49 shorter events, 19.8 us)
Async XLA Ops:
  0.0 95.3 %collective-permute-start.15 = (bf16[1024,2048]{1,0:T(8,128)(2,1)}, bf16[1024,2048]{1,0:T(8,128)(2,1)}, u32[]{:S(2)}, u32[]{:S(2)}) collective-permute-start(bf16[1024,2048]{1,0:T(8,128)(2,1)} %refs_2_.1), channel_id=1, source_target_pairs={{0,2},{1,3},{2,0},{3,1},{4,5},{5,6},{6,7},{7,4},{8,10},{9,11},{10,... | collective-permute-start | bytes 12582920 | tf_op jit(solution)/shard_map/ppermute | solution.py:466
  3.4 91.9 %collective-permute-start.16 = (bf16[1024,2048]{1,0:T(8,128)(2,1)}, bf16[1024,2048]{1,0:T(8,128)(2,1)}, u32[]{:S(2)}, u32[]{:S(2)}) collective-permute-start(bf16[1024,2048]{1,0:T(8,128)(2,1)} %refs_2_.1), channel_id=1, source_target_pairs={{0,32},{1,33},{2,34},{3,35},{4,7},{5,4},{6,5},{7,6},{8,40},{9,41},... | collective-permute-start | bytes 12582920 | tf_op jit(solution)/shard_map/ppermute | solution.py:467
  6.3 83.2 %copy-start = (bf16[1024,1024]{1,0:T(8,128)(2,1)S(1)}, bf16[1024,1024]{1,0:T(8,128)(2,1)}, u32[]{:S(2)}) copy-start(bf16[1024,1024]{1,0:T(8,128)(2,1)} %gate_ref.3) | copy-start | bytes 6291460
  6.3 83.2 %copy-start.7 = (f32[128]{0:T(128)S(1)}, f32[128]{0:T(128)}, u32[]{:S(2)}) copy-start(f32[128]{0:T(128)} %param.20) | copy-start | bytes 1540
  6.3 2.5 %collective-permute-start = (bf16[8,2048]{1,0:T(8,128)(2,1)}, bf16[8,2048]{1,0:T(8,128)(2,1)S(1)}, u32[]{:S(2)}, u32[]{:S(2)}) collective-permute-start(bf16[8,2048]{1,0:T(8,128)(2,1)} %rim.1), channel_id=1, source_target_pairs={{0,4},{4,8},{8,12},{12,16},{16,20},{20,24},{24,28},{28,32},{32,36}... | collective-permute-start | bytes 98312 | tf_op jit(solution)/shard_map/ppermute | solution.py:465
  48.0 4.5 %collective-permute-start.1 = (f32[4,128,256]{2,1,0:T(8,128)S(1)}, f32[4,128,256]{2,1,0:T(8,128)S(1)}, u32[]{:S(2)}, u32[]{:S(2)}) collective-permute-start(f32[4,128,256]{2,1,0:T(8,128)S(1)} %get-tuple-element.40), channel_id=1, source_target_pairs={{0,4},{4,0},{8,12},{12,8},{16,20},{20,16},{24,28},{28,24},{32,36},... | collective-permute-start | bytes 1572872 | tf_op jit(solution)/shard_map/ppermute | solution.py:457
  53.5 8.5 %collective-permute-start.2 = (f32[128,256]{1,0:T(8,128)S(1)}, f32[128,256]{1,0:T(8,128)S(1)}, u32[]{:S(2)}, u32[]{:S(2)}) collective-permute-start(f32[128,256]{1,0:T(8,128)S(1)} %get-tuple-element.42), channel_id=1, source_target_pairs={{0,8},{4,12},{8,16},{12,20},{16,24},{20,28},{24,0},{28,4},{32,40},... | collective-permute-start | bytes 393224 | tf_op jit(solution)/shard_map/ppermute | solution.py:457
  56.0 9.9 %collective-permute-start.3 = (f32[128,256]{1,0:T(8,128)S(1)}, f32[128,256]{1,0:T(8,128)S(1)}, u32[]{:S(2)}, u32[]{:S(2)}) collective-permute-start(f32[128,256]{1,0:T(8,128)S(1)} %get-tuple-element.43), channel_id=1, source_target_pairs={{0,16},{4,20},{8,24},{12,28},{16,0},{20,4},{24,8},{28,12},{32,48},... | collective-permute-start | bytes 393224 | tf_op jit(solution)/shard_map/ppermute | solution.py:457
  59.6 6.3 %collective-permute-start.4 = (f32[128,256]{1,0:T(8,128)S(1)}, f32[128,256]{1,0:T(8,128)S(1)}, u32[]{:S(2)}, u32[]{:S(2)}) collective-permute-start(f32[128,256]{1,0:T(8,128)S(1)} %get-tuple-element.44), channel_id=1, source_target_pairs={{0,24},{4,28},{8,0},{12,4},{16,8},{20,12},{24,16},{28,20},{32,56},... | collective-permute-start | bytes 393224 | tf_op jit(solution)/shard_map/ppermute | solution.py:457
  67.0 7.6 %collective-permute-start.5 = (f32[128,256]{1,0:T(8,128)S(1)}, f32[128,256]{1,0:T(8,128)S(1)}, u32[]{:S(2)}, u32[]{:S(2)}) collective-permute-start(f32[128,256]{1,0:T(8,128)S(1)} %get-tuple-element.45.a0), channel_id=1, source_target_pairs={{0,32},{4,36},{8,40},{12,44},{16,48},{20,52},{24,56},{28,60},{32,6... | collective-permute-start | bytes 393224 | tf_op jit(solution)/shard_map/ppermute | solution.py:457
  69.3 7.1 %collective-permute-start.6 = (f32[128,256]{1,0:T(8,128)S(1)}, f32[128,256]{1,0:T(8,128)S(1)}, u32[]{:S(2)}, u32[]{:S(2)}) collective-permute-start(f32[128,256]{1,0:T(8,128)S(1)} %get-tuple-element.45.a0), channel_id=1, source_target_pairs={{0,64},{4,68},{8,72},{12,76},{16,80},{20,84},{24,88},{28,92},{32,9... | collective-permute-start | bytes 393224 | tf_op jit(solution)/shard_map/ppermute | solution.py:457
  71.1 5.4 %collective-permute-start.7 = (f32[128,256]{1,0:T(8,128)S(1)}, f32[128,256]{1,0:T(8,128)S(1)}, u32[]{:S(2)}, u32[]{:S(2)}) collective-permute-start(f32[128,256]{1,0:T(8,128)S(1)} %get-tuple-element.45.a0), channel_id=1, source_target_pairs={{0,96},{4,100},{8,104},{12,108},{16,112},{20,116},{24,120},{28,124... | collective-permute-start | bytes 393224 | tf_op jit(solution)/shard_map/ppermute | solution.py:457
  77.7 6.6 %collective-permute-start.8 = (f32[128,128]{1,0:T(8,128)S(1)}, f32[128,128]{1,0:T(8,128)S(1)}, u32[]{:S(2)}, u32[]{:S(2)}) collective-permute-start(f32[128,128]{1,0:T(8,128)S(1)} %get-tuple-element.48), channel_id=1, source_target_pairs={{0,8},{4,12},{8,16},{12,20},{16,24},{20,28},{24,0},{28,4},{32,40},... | collective-permute-start | bytes 196616 | tf_op jit(solution)/shard_map/ppermute | solution.py:457
  79.3 6.4 %collective-permute-start.9 = (f32[128,128]{1,0:T(8,128)S(1)}, f32[128,128]{1,0:T(8,128)S(1)}, u32[]{:S(2)}, u32[]{:S(2)}) collective-permute-start(f32[128,128]{1,0:T(8,128)S(1)} %get-tuple-element.49), channel_id=1, source_target_pairs={{0,16},{4,20},{8,24},{12,28},{16,0},{20,4},{24,8},{28,12},{32,48},... | collective-permute-start | bytes 196616 | tf_op jit(solution)/shard_map/ppermute | solution.py:457
  82.8 4.3 %collective-permute-start.10 = (f32[128,128]{1,0:T(8,128)S(1)}, f32[128,128]{1,0:T(8,128)S(1)}, u32[]{:S(2)}, u32[]{:S(2)}) collective-permute-start(f32[128,128]{1,0:T(8,128)S(1)} %get-tuple-element.50), channel_id=1, source_target_pairs={{0,24},{4,28},{8,0},{12,4},{16,8},{20,12},{24,16},{28,20},{32,56},... | collective-permute-start | bytes 196616 | tf_op jit(solution)/shard_map/ppermute | solution.py:457
  87.9 1.6 %collective-permute-start.11 = (f32[4,128,128]{2,1,0:T(8,128)S(1)}, f32[4,128,128]{2,1,0:T(8,128)S(1)}, u32[]{:S(2)}, u32[]{:S(2)}) collective-permute-start(f32[4,128,128]{2,1,0:T(8,128)S(1)} %get-tuple-element.53), channel_id=1, source_target_pairs={{0,4},{4,0},{8,12},{12,8},{16,20},{20,16},{24,28},{28,24},{32,36},... | collective-permute-start | bytes 786440 | tf_op jit(solution)/shard_map/ppermute | solution.py:457
  95.3 29.6 %collective-permute-start.17 = (bf16[1024,2048]{1,0:T(8,128)(2,1)}, bf16[1024,2048]{1,0:T(8,128)(2,1)S(1)}, u32[]{:S(2)}, u32[]{:S(2)}) collective-permute-start(bf16[1024,2048]{1,0:T(8,128)(2,1)} %collective-permute-done.15.refs_0_), channel_id=1, source_target_pairs={{0,4},{4,0},{8,12},{12,8},{16,20},{20,16},{24,28},{28,24},{32,36},... | collective-permute-start | bytes 12582920 | tf_op jit(solution)/shard_map/ppermute | solution.py:457
  95.3 29.6 %collective-permute-start.18 = (bf16[1024,2048]{1,0:T(8,128)(2,1)}, bf16[1024,2048]{1,0:T(8,128)(2,1)S(1)}, u32[]{:S(2)}, u32[]{:S(2)}) collective-permute-start(bf16[1024,2048]{1,0:T(8,128)(2,1)} %collective-permute-done.16.refs_1_), channel_id=1, source_target_pairs={{0,4},{4,0},{8,12},{12,8},{16,20},{20,16},{24,28},{28,24},{32,36},... | collective-permute-start | bytes 12582920 | tf_op jit(solution)/shard_map/ppermute | solution.py:457
  101.0 14.5 %collective-permute-start.19 = (bf16[256,512]{1,0:T(8,128)(2,1)S(1)}, bf16[256,512]{1,0:T(8,128)(2,1)S(1)}, u32[]{:S(2)}, u32[]{:S(2)}) collective-permute-start(bf16[256,512]{1,0:T(8,128)(2,1)S(1)} %get-tuple-element.65), channel_id=1, source_target_pairs={{0,1},{1,2},{2,3},{3,0},{4,5},{5,6},{6,7},{7,4},{8,9},{9,10},{10,1... | collective-permute-start | bytes 786440 | tf_op jit(solution)/shard_map/ppermute | solution.py:458
  102.2 13.3 %collective-permute-start.20 = (bf16[256,512]{1,0:T(8,128)(2,1)S(1)}, bf16[256,512]{1,0:T(8,128)(2,1)S(1)}, u32[]{:S(2)}, u32[]{:S(2)}) collective-permute-start(bf16[256,512]{1,0:T(8,128)(2,1)S(1)} %get-tuple-element.66), channel_id=1, source_target_pairs={{0,3},{1,0},{2,1},{3,2},{4,7},{5,4},{6,5},{7,6},{8,11},{9,8},{10,9... | collective-permute-start | bytes 786440 | tf_op jit(solution)/shard_map/ppermute | solution.py:458
  104.3 15.3 %collective-permute-start.21 = (bf16[256,512]{1,0:T(8,128)(2,1)S(1)}, bf16[256,512]{1,0:T(8,128)(2,1)S(1)}, u32[]{:S(2)}, u32[]{:S(2)}) collective-permute-start(bf16[256,512]{1,0:T(8,128)(2,1)S(1)} %get-tuple-element.67), channel_id=1, source_target_pairs={{0,2},{1,3},{2,0},{3,1},{4,6},{5,7},{6,4},{7,5},{8,10},{9,11},{10,... | collective-permute-start | bytes 786440 | tf_op jit(solution)/shard_map/ppermute | solution.py:458
  115.5 13.2 %collective-permute-start.12 = (bf16[256,512]{1,0:T(8,128)(2,1)S(1)}, bf16[256,512]{1,0:T(8,128)(2,1)S(1)}, u32[]{:S(2)}, u32[]{:S(2)}) collective-permute-start(bf16[256,512]{1,0:T(8,128)(2,1)S(1)} %get-tuple-element.54), channel_id=1, source_target_pairs={{0,1},{1,2},{2,3},{3,0},{4,5},{5,6},{6,7},{7,4},{8,9},{9,10},{10,1... | collective-permute-start | bytes 786440 | tf_op jit(solution)/shard_map/ppermute | solution.py:458
  115.5 13.2 %collective-permute-start.13 = (bf16[256,512]{1,0:T(8,128)(2,1)S(1)}, bf16[256,512]{1,0:T(8,128)(2,1)S(1)}, u32[]{:S(2)}, u32[]{:S(2)}) collective-permute-start(bf16[256,512]{1,0:T(8,128)(2,1)S(1)} %get-tuple-element.55), channel_id=1, source_target_pairs={{0,3},{1,0},{2,1},{3,2},{4,7},{5,4},{6,5},{7,6},{8,11},{9,8},{10,9... | collective-permute-start | bytes 786440 | tf_op jit(solution)/shard_map/ppermute | solution.py:458
  119.6 9.1 %collective-permute-start.14 = (bf16[256,512]{1,0:T(8,128)(2,1)S(1)}, bf16[256,512]{1,0:T(8,128)(2,1)S(1)}, u32[]{:S(2)}, u32[]{:S(2)}) collective-permute-start(bf16[256,512]{1,0:T(8,128)(2,1)S(1)} %get-tuple-element.56), channel_id=1, source_target_pairs={{0,2},{1,3},{2,0},{3,1},{4,6},{5,7},{6,4},{7,5},{8,10},{9,11},{10,... | collective-permute-start | bytes 786440 | tf_op jit(solution)/shard_map/ppermute | solution.py:458
  (6 other events, 68.3 us)

commit v2 on v1

--- a/solution.py
+++ b/solution.py
@@ -330,82 +330,116 @@
     )(pos, base, maps, kept, got, gate, gain)
 
 
-def project_kernel(pos, *refs, starts, picks, held, count, extra, final):
-    ys, ws = refs[:count], refs[count : count + held]
-    here, there = [ws[i] for i in picks[0]], [ws[i] for i in picks[1]]
-    acc_ref = refs[count + held] if extra else None
-    out_ref, *more = refs[count + held + extra :]
-    depth = ys[0].shape[1]
-    tile = 512
+def own_kernel(ya, yb, w, out_ref):
+    depth = ya.shape[1]
+    for c in range(0, out_ref.shape[1], 512):
+        cols = slice(c, c + 512)
+        out_ref[:, cols] = mxu(ya[...], w[:depth, cols]) + mxu(yb[...], w[depth:, cols])
+
+
+def run_own(ya, yb, weight):
+    vmem = pl.BlockSpec(memory_space=pltpu.VMEM)
+    return pl.pallas_call(
+        own_kernel,
+        in_specs=[vmem] * 3,
+        out_specs=vmem,
+        out_shape=jax.ShapeDtypeStruct((ya.shape[0], weight.shape[1]), F32),
+        compiler_params=pltpu.CompilerParams(vmem_limit_bytes=LIMIT),
+        name="own",
+    )(ya, yb, weight)
+
+
+def project_kernel(pos, y1, y3, y2, mine, theirs, q_mine, n_mine, q_theirs, n_theirs, acc_ref, out_ref, *more,
+                   part, final):
+    depth, tile = y1.shape[1], 512
     tiles = out_ref.shape[1] // tile
-
-    def sweep(ws):
+    rows = slice(part * depth, (part + 1) * depth)
+    size = q_mine.shape[0]
+    parity = pos[part] % 2
+    first = pl.ds(pl.multiple_of(parity * size, size), size)
+    second = pl.ds(pl.multiple_of((1 - parity) * size, size), size)
+
+    def store(t):
+        return pltpu.make_async_copy(more[0].at[t], out_ref.at[:, pl.ds(t * tile, tile)], more[1].at[t])
+
+    def sweep(w1, w3, near, far):
         for t in range(tiles):
             cols = slice(t * tile, (t + 1) * tile)
-            total = acc_ref[:, cols] if extra else None
-            for p in range(count):
-                term = mxu(ys[p][...], ws[p][starts[p] : starts[p] + depth, cols])
-                total = term if total is None else total + term
+            total = acc_ref[:, cols] + mxu(y1[...], w1[rows, cols]) + mxu(y3[...], w3[rows, cols])
+            total = total + mxu(y2[:, first], near[:, cols]) + mxu(y2[:, second], far[:, cols])
             if final:
                 more[0][t] = total.astype(BF16)
                 store(t).start()
             else:
                 out_ref[:, cols] = total
 
-    def store(t):
-        return pltpu.make_async_copy(more[0].at[t], out_ref.at[:, pl.ds(t * tile, tile)], more[1].at[t])
-
-    if picks[0] == picks[1]:
-        sweep(here)
-    else:
-        pl.when(pos[2] == 0)(lambda: sweep(here))
-        pl.when(pos[2] != 0)(lambda: sweep(there))
+    for core, (w1, w3) in enumerate(((mine, theirs), (theirs, mine))):
+        near, far = (q_mine, n_mine) if core == part else (q_theirs, n_theirs)
+        pl.when(pos[2] == core)(functools.partial(sweep, w1, w3, near, far))
     if final:
         for t in range(tiles):
             store(t).wait()
 
 
-def project(pos, starts, ys, weights, picks, acc, dtype):
-    rows, _ = ys[0].shape
-    width = weights[0].shape[1]
-    count = len(ys)
-    final = dtype == BF16
+def project(pos, part, ys, weights, acc, final):
+    rows, width = acc.shape
     vmem, hbm = pl.BlockSpec(memory_space=pltpu.VMEM), pl.BlockSpec(memory_space=pl.ANY)
-    accs = [] if acc is None else [acc]
-    return pl.pallas_call(
-        functools.partial(project_kernel, starts=starts, picks=picks, held=len(weights), count=count, extra=len(accs), final=final),
-        in_specs=[pl.BlockSpec(memory_space=pltpu.SMEM)] + [vmem] * (count + len(weights) + len(accs)),
+    dtype = BF16 if final else F32
+    return pl.pallas_call(
+        functools.partial(project_kernel, part=part, final=final),
+        in_specs=[pl.BlockSpec(memory_space=pltpu.SMEM)] + [vmem] * 10,
         out_specs=hbm if final else vmem,
         out_shape=jax.ShapeDtypeStruct((rows, width), dtype),
         scratch_shapes=[pltpu.VMEM((width // 512, rows, 512), dtype), pltpu.SemaphoreType.DMA((width // 512,))] * final,
         compiler_params=pltpu.CompilerParams(vmem_limit_bytes=14 << 20),
-    )(pos, *ys, *weights, *accs)
-
-
-def fetch_kernel(*refs):
-    sem = refs[-1]
-    copies = []
-    for i in range(2):
-        rows = refs[i].shape[0] // 4
-        for j in range(4):
-            part = pl.ds(j * rows, rows)
-            copies.append(pltpu.make_async_copy(refs[i].at[part], refs[2 + i].at[part], sem.at[i, j]))
+    )(pos, *ys, *weights, acc)
+
+
+def quarter_kernel(pos, w, out_ref, sem):
+    rows = out_ref.shape[0]
+    side = jnp.where(pos[2] == 0, pos[0], pos[1]) % 2
+    top = pl.multiple_of((pos[2] * 2 + side) * rows, rows)
+    piece = rows // 4
+    copies = [pltpu.make_async_copy(w.at[pl.ds(top + i * piece, piece)], out_ref.at[pl.ds(i * piece, piece)], sem.at[i])
+              for i in range(4)]
     for c in copies:
         c.start()
     for c in copies:
         c.wait()
 
 
-def run_fetch(*arrays):
+def run_quarter(pos, weight):
+    return pl.pallas_call(
+        quarter_kernel,
+        in_specs=[pl.BlockSpec(memory_space=pltpu.SMEM), pl.BlockSpec(memory_space=pl.ANY)],
+        out_specs=pl.BlockSpec(memory_space=pltpu.VMEM),
+        out_shape=jax.ShapeDtypeStruct((weight.shape[0] // 4, weight.shape[1]), BF16),
+        scratch_shapes=[pltpu.SemaphoreType.DMA((4,))],
+        compiler_params=pltpu.CompilerParams(vmem_limit_bytes=LIMIT),
+        name="quarter",
+    )(pos, weight)
+
+
+def fetch_kernel(w, out_ref, sem):
+    rows = w.shape[0] // 8
+    parts = [pl.ds(i * rows, rows) for i in range(8)]
+    copies = [pltpu.make_async_copy(w.at[p], out_ref.at[p], sem.at[i]) for i, p in enumerate(parts)]
+    for c in copies:
+        c.start()
+    for c in copies:
+        c.wait()
+
+
+def run_fetch(w):
     return pl.pallas_call(
         fetch_kernel,
-        in_specs=[pl.BlockSpec(memory_space=pl.ANY)] * 2,
-        out_specs=[pl.BlockSpec(memory_space=pltpu.VMEM)] * 2,
-        out_shape=[jax.ShapeDtypeStruct(a.shape, a.dtype) for a in arrays],
-        scratch_shapes=[pltpu.SemaphoreType.DMA((2, 4))],
+        in_specs=[pl.BlockSpec(memory_space=pl.ANY)],
+        out_specs=pl.BlockSpec(memory_space=pltpu.VMEM),
+        out_shape=jax.ShapeDtypeStruct(w.shape, w.dtype),
+        scratch_shapes=[pltpu.SemaphoreType.DMA((8,))],
         compiler_params=pltpu.CompilerParams(vmem_limit_bytes=LIMIT),
         name="fetch",
-    )(*arrays)
+    )(w)
 
 
 def rim_kernel(q, k, v, out_ref, sem):
@@ -428,6 +462,7 @@
         out_specs=pl.BlockSpec(memory_space=pltpu.VMEM),
         out_shape=jax.ShapeDtypeStruct((8, q.shape[1] + k.shape[1] + v.shape[1]), BF16),
         scratch_shapes=[pltpu.SemaphoreType.DMA((3,))],
+        compiler_params=pltpu.CompilerParams(vmem_limit_bytes=LIMIT),
         name="rim",
     )(q, k, v)
 
@@ -440,11 +475,14 @@
     return [(i, dest(i)) for i in range(X_CHIPS * Z_CHIPS * CORES)]
 
 
-def mesh_route(n_ctx, heads, moves):
-    row = Z_CHIPS * CORES
+def mesh_route(n_ctx, heads, turns):
     pairs = [(c, h) for c in range(n_ctx) for h in range(heads)]
-    dest = lambda c, h, dx, dy: (c + dx * row) % n_ctx * heads + (h + dy) % heads
-    return [(c * heads + h, dest(c, h, *moves[c % CORES])) for c, h in pairs]
+    return [(c * heads + h, c * heads + (h + turns[c % CORES]) % heads) for c, h in pairs]
+
+
+def beside_route(n_ctx):
+    flip = (Z_CHIPS * CORES, CORES)
+    return [(c, c ^ flip[c % CORES]) for c in range(n_ctx)]
 
 
 def shards(query_raw, key_raw, value_raw, gate_branch, gate_code, beta_code,
@@ -461,17 +499,18 @@
 
     n_ctx = lax.axis_size("ctx")
     raws = [pltpu.with_memory_space_constraint(a, pltpu.HBM) for a in (query_raw, key_raw, value_raw)]
-    w_rows = out_weight.shape[0] // CORES
     halo = lax.ppermute(run_rim(*raws), "ctx", [(i, i + 1) for i in range(n_ctx - 1)])
-    w_first = lax.ppermute(out_weight, ("ctx", "head"), mesh_route(n_ctx, heads, ((0, 2), (0, 1))))
-    w_second = lax.ppermute(out_weight, ("ctx", "head"), mesh_route(n_ctx, heads, ((1, 0), (0, 3))))
+    w_full = lax.ppermute(out_weight, ("ctx", "head"), mesh_route(n_ctx, heads, (1, 3)))
+    w_near = turn(run_quarter(pos, out_weight), 2)
 
     base, maps, kept, away = run_scan(pos, *raws, gate_code.T, beta_code.T, halo,
                                       conv_query, conv_key, conv_value)
 
     line, full = (HD, 2 * HD), (Z_CHIPS, HD, 2 * HD)
     early, *both = vmem_call(pair_kernel, [full] + [line] * 4, [full], pos, kept, send(away, 0, 0, 1))
+    *both, w_local = barrier((*both, out_weight))
     lines = [both[0]] + [send(both[d], 0, d, 0) for d in range(1, Z_CHIPS)]
+    *lines, w_local = barrier((*lines, run_fetch(w_local)))
     pre, tot = vmem_call(prefix_kernel, [full, line], [full], pos, *lines)
     tots = [tot] + [send(tot, d, 0, 0) for d in range(1, X_CHIPS)]
     entry = vmem_call(entry_kernel, [(HD, HD)] * 4, [full, (Z_CHIPS, HD, HD)], pos, *tots, pre)
@@ -482,16 +521,18 @@
     gain = norm_gain.reshape(1, HD)
     y_a = run_out(pos, base, maps, own, got, gate_branch, gain, 0)
     a_got = [turn(y_a[d], d) for d in hops]
+    _, w_full, w_near = barrier((y_a[0], w_full, w_near))
+    w_far = lax.ppermute(w_near, "ctx", beside_route(n_ctx))
+    near_there, full_there = send(w_near, 0, 0, 1), send(w_full, 0, 0, 1)
     y_b = run_out(pos, base, maps, own, got, gate_branch, gain, 1)
     b_got = [turn(y_b[d], d) for d in hops]
-    _, w_first, w_second = barrier((y_b[0], w_first, w_second))
-    swap_first, swap_second = send(w_first, 0, 0, 1), send(w_second, 0, 0, 1)
-    acc = project(pos, (0, w_rows), [y_a[0], y_b[0]], [out_weight], ((0, 0),) * 2, None, F32)
-    acc, w_first, w_second = barrier((acc, w_first, w_second))
-    held = [*run_fetch(w_first, w_second), swap_first, swap_second]
-    picks = ((2, 3, 0), (0, 1, 2))
-    acc = project(pos, (0,) * 3, a_got, held, picks, acc, F32)
-    return project(pos, (w_rows,) * 3, b_got, held, picks, acc, BF16)
+    acc = run_own(y_a[0], y_b[0], w_local)
+    acc, w_far = barrier((acc, w_far))
+    far_there = send(w_far, 0, 0, 1)
+    acc, w_kept = barrier((acc, w_full))
+    weights = [run_fetch(w_kept), full_there, w_near, w_far, near_there, far_there]
+    acc = project(pos, 0, a_got, weights, acc, False)
+    return project(pos, 1, b_got, weights, acc, True)
 
 
 def solution(mesh):

time: 132 us -> 143 us (1.083)
  the two profiles are of different devices: /device:TPU:0 before, /device:TPU:1 now
where the time goes in v2:
time: 143 us; the launch traced here: 142 us
  Pallas kernels  64.5 us (45%)
  waiting for transfers between devices  41.6 us (29%)
  starting transfers between devices  34.9 us (24%)
    pallas_call x1, Pallas kernels, run_scan(): pl.pallas_call(scan_kernel, grid=(rows // BLOCK,), in_specs=[pl.BlockSpec...  39.4 us
    ppermute x14, starting transfers between devices, shards(): send = lambda a, dx, dz, dc: lax.ppermute(a, 'ctx', ctx_route(dx, dz, dc))  21.5 us
    ppermute x7, waiting for transfers between devices, shards(): lax.ppermute(a, 'head', [(i, (i + d) % heads) for i in range(heads)])  20.1 us
    ppermute x14, waiting for transfers between devices, shards(): send = lambda a, dx, dz, dc: lax.ppermute(a, 'ctx', ctx_route(dx, dz, dc))  14.5 us
    pallas_call x2, Pallas kernels, run_out(): pl.pallas_call(functools.partial(out_kernel, part=part), in_specs=[pl.Blo...  10.3 us
    ppermute x7, starting transfers between devices, shards(): lax.ppermute(a, 'head', [(i, (i + d) % heads) for i in range(heads)])  6.86 us
    ppermute x1, waiting for transfers between devices, shards(): w_far = lax.ppermute(w_near, 'ctx', beside_route(n_ctx))  6.15 us
    pallas_call x2, Pallas kernels, project(): pl.pallas_call(functools.partial(project_kernel, part=part, final=final),...  5.51 us
  transfers between devices with their start and end apart: 24, of which 15 were waited for; matrix products, arithmetic and copies ran while one was open for 0% of the time, Pallas kernels for 43%

profile of v2, /device:TPU:1, one launch (start us, length us, event | category | flops | bytes accessed | tf_op | source)
XLA Modules:
  0.0 141.6 jit_solution(11770253223236322357)
XLA Ops:
  0.0 3.6 %collective-permute-start.15 = (bf16[1024,2048]{1,0:T(8,128)(2,1)}, bf16[1024,2048]{1,0:T(8,128)(2,1)}, u32[]{:S(2)}, u32[]{:S(2)}) collective-permute-start(bf16[1024,2048]{1,0:T(8,128)(2,1)} %w.2), channel_id=1, source_target_pairs={{0,1},{1,2},{2,3},{3,0},{4,7},{5,4},{6,5},{7,6},{8,9},{9,10},{10,1... | collective-permute-start | bytes 12582920 | tf_op jit(solution)/shard_map/ppermute | solution.py:503
  4.4 2.9 %collective-permute-start = (bf16[8,2048]{1,0:T(8,128)(2,1)S(1)}, bf16[8,2048]{1,0:T(8,128)(2,1)S(1)}, u32[]{:S(2)}, u32[]{:S(2)}) collective-permute-start(bf16[8,2048]{1,0:T(8,128)(2,1)S(1)} %rim.1), channel_id=1, source_target_pairs={{0,4},{4,8},{8,12},{12,16},{16,20},{20,24},{24,28},{28,32},{32,36}... | collective-permute-start | bytes 98312 | tf_op jit(solution)/shard_map/ppermute | solution.py:502
  8.4 39.4 %scan.1 = (f32[1024,1024]{1,0:T(8,128)S(1)}, bf16[1024,2048]{1,0:T(8,128)(2,1)S(1)}, f32[4,128,256]{2,1,0:T(8,128)S(1)}, f32[4,128,256]{2,1,0:T(8,128)S(1)}) custom-call(s32[4]{0:T(128)S(1)} %pad_add_fusion.pos, bf16[1024,512]{1,0:T(8,128)(2,1)} %q_ref.1, bf16[1024,512]{1,0:T(8,128)(2,1)} %k_ref.1, bf16[1024,1024]{1,0:T(8,128)(2,1)} %v_ref.1, ...), custom_call_target="tpu_custom_call" | custom-call | tf_op jit(solution)/shard_map/scan/pallas_call | solution.py:203
  48.6 2.7 %collective-permute-start.16 = (bf16[256,2048]{1,0:T(8,128)(2,1)S(1)}, bf16[256,2048]{1,0:T(8,128)(2,1)S(1)}, u32[]{:S(2)}, u32[]{:S(2)}) collective-permute-start(bf16[256,2048]{1,0:T(8,128)(2,1)S(1)} %quarter.1), channel_id=1, source_target_pairs={{0,2},{1,3},{2,0},{3,1},{4,6},{5,7},{6,4},{7,5},{8,10},{9,11},{10,... | collective-permute-start | bytes 3145736 | tf_op jit(solution)/shard_map/ppermute | solution.py:496
  52.3 2.2 %collective-permute-start.2 = (f32[128,256]{1,0:T(8,128)S(1)}, f32[128,256]{1,0:T(8,128)S(1)}, u32[]{:S(2)}, u32[]{:S(2)}) collective-permute-start(f32[128,256]{1,0:T(8,128)S(1)} %get-tuple-element.55), channel_id=1, source_target_pairs={{0,8},{4,12},{8,16},{12,20},{16,24},{20,28},{24,0},{28,4},{32,40},... | collective-permute-start | bytes 393224 | tf_op jit(solution)/shard_map/ppermute | solution.py:495
  54.5 3.3 %collective-permute-start.3 = (f32[128,256]{1,0:T(8,128)S(1)}, f32[128,256]{1,0:T(8,128)S(1)}, u32[]{:S(2)}, u32[]{:S(2)}) collective-permute-start(f32[128,256]{1,0:T(8,128)S(1)} %get-tuple-element.56), channel_id=1, source_target_pairs={{0,16},{4,20},{8,24},{12,28},{16,0},{20,4},{24,8},{28,12},{32,48},... | collective-permute-start | bytes 393224 | tf_op jit(solution)/shard_map/ppermute | solution.py:495
  60.2 3.7 %collective-permute-done.3.a2 = f32[128,256]{1,0:T(8,128)S(1)} collective-permute-done((f32[128,256]{1,0:T(8,128)S(1)}, f32[128,256]{1,0:T(8,128)S(1)}, u32[]{:S(2)}, u32[]{:S(2)}) %collective-permute-start.3) | collective-permute-done | bytes 131104 | tf_op jit(solution)/shard_map/ppermute | solution.py:495
  66.4 2.5 %collective-permute-start.6 = (f32[128,256]{1,0:T(8,128)S(1)}, f32[128,256]{1,0:T(8,128)S(1)}, u32[]{:S(2)}, u32[]{:S(2)}) collective-permute-start(f32[128,256]{1,0:T(8,128)S(1)} %get-tuple-element.63.a0), channel_id=1, source_target_pairs={{0,64},{4,68},{8,72},{12,76},{16,80},{20,84},{24,88},{28,92},{32,9... | collective-permute-start | bytes 393224 | tf_op jit(solution)/shard_map/ppermute | solution.py:495
  70.4 3.4 %collective-permute-done.6.a2 = f32[128,256]{1,0:T(8,128)S(1)} collective-permute-done((f32[128,256]{1,0:T(8,128)S(1)}, f32[128,256]{1,0:T(8,128)S(1)}, u32[]{:S(2)}, u32[]{:S(2)}) %collective-permute-start.6) | collective-permute-done | bytes 131104 | tf_op jit(solution)/shard_map/ppermute | solution.py:495
  75.6 2.3 %collective-permute-start.8 = (f32[128,128]{1,0:T(8,128)S(1)}, f32[128,128]{1,0:T(8,128)S(1)}, u32[]{:S(2)}, u32[]{:S(2)}) collective-permute-start(f32[128,128]{1,0:T(8,128)S(1)} %get-tuple-element.66), channel_id=1, source_target_pairs={{0,8},{4,12},{8,16},{12,20},{16,24},{20,28},{24,0},{28,4},{32,40},... | collective-permute-start | bytes 196616 | tf_op jit(solution)/shard_map/ppermute | solution.py:495
  77.9 2.7 %collective-permute-start.9 = (f32[128,128]{1,0:T(8,128)S(1)}, f32[128,128]{1,0:T(8,128)S(1)}, u32[]{:S(2)}, u32[]{:S(2)}) collective-permute-start(f32[128,128]{1,0:T(8,128)S(1)} %get-tuple-element.67), channel_id=1, source_target_pairs={{0,16},{4,20},{8,24},{12,28},{16,0},{20,4},{24,8},{28,12},{32,48},... | collective-permute-start | bytes 196616 | tf_op jit(solution)/shard_map/ppermute | solution.py:495
  81.0 2.0 %collective-permute-done.9.a2 = f32[128,128]{1,0:T(8,128)S(1)} collective-permute-done((f32[128,128]{1,0:T(8,128)S(1)}, f32[128,128]{1,0:T(8,128)S(1)}, u32[]{:S(2)}, u32[]{:S(2)}) %collective-permute-start.9) | collective-permute-done | bytes 65568 | tf_op jit(solution)/shard_map/ppermute | solution.py:495
  83.0 1.5 %collective-permute-done.10.a3 = f32[128,128]{1,0:T(8,128)S(1)} collective-permute-done((f32[128,128]{1,0:T(8,128)S(1)}, f32[128,128]{1,0:T(8,128)S(1)}, u32[]{:S(2)}, u32[]{:S(2)}) %collective-permute-start.10) | collective-permute-done | bytes 65568 | tf_op jit(solution)/shard_map/ppermute | solution.py:495
  85.3 2.3 %collective-permute-start.11 = (f32[4,128,128]{2,1,0:T(8,128)S(1)}, f32[4,128,128]{2,1,0:T(8,128)S(1)}, u32[]{:S(2)}, u32[]{:S(2)}) collective-permute-start(f32[4,128,128]{2,1,0:T(8,128)S(1)} %get-tuple-element.71), channel_id=1, source_target_pairs={{0,4},{4,0},{8,12},{12,8},{16,20},{20,16},{24,28},{28,24},{32,36},... | collective-permute-start | bytes 786440 | tf_op jit(solution)/shard_map/ppermute | solution.py:495
  88.8 5.1 %shard_map.114 = (bf16[256,512]{1,0:T(8,128)(2,1)S(1)}, bf16[256,512]{1,0:T(8,128)(2,1)S(1)}, bf16[256,512]{1,0:T(8,128)(2,1)S(1)}, bf16[256,512]{1,0:T(8,128)(2,1)S(1)}) custom-call(s32[4]{0:T(128)S(1)} %pad_add_fusion.pos, f32[1024,1024]{1,0:T(8,128)S(1)} %get-tuple-element.46.base_ref, bf16[1024,2048]{1,0:T(8,128)(2,1)S(1)} %get-tuple-element.47.map_ref, ...), custom_call_target="tpu_custom_call" | custom-call | tf_op jit(solution)/shard_map/pallas_call | solution.py:323
  95.8 5.2 %shard_map.113 = (bf16[256,512]{1,0:T(8,128)(2,1)S(1)}, bf16[256,512]{1,0:T(8,128)(2,1)S(1)}, bf16[256,512]{1,0:T(8,128)(2,1)S(1)}, bf16[256,512]{1,0:T(8,128)(2,1)S(1)}) custom-call(s32[4]{0:T(128)S(1)} %pad_add_fusion.pos, f32[1024,1024]{1,0:T(8,128)S(1)} %get-tuple-element.46.base_ref, bf16[1024,2048]{1,0:T(8,128)(2,1)S(1)} %get-tuple-element.47.map_ref, ...), custom_call_target="tpu_custom_call" | custom-call | tf_op jit(solution)/shard_map/pallas_call | solution.py:323
  102.3 6.1 %collective-permute-done.17.n_mine = bf16[256,2048]{1,0:T(8,128)(2,1)S(1)} collective-permute-done((bf16[256,2048]{1,0:T(8,128)(2,1)S(1)}, bf16[256,2048]{1,0:T(8,128)(2,1)S(1)}, u32[]{:S(2)}, u32[]{:S(2)}) %collective-permute-start.17) | collective-permute-done | bytes 1048608 | tf_op jit(solution)/shard_map/ppermute | solution.py:525
  109.4 2.7 %collective-permute-start.22 = (bf16[256,512]{1,0:T(8,128)(2,1)S(1)}, bf16[256,512]{1,0:T(8,128)(2,1)S(1)}, u32[]{:S(2)}, u32[]{:S(2)}) collective-permute-start(bf16[256,512]{1,0:T(8,128)(2,1)S(1)} %get-tuple-element.84), channel_id=1, source_target_pairs={{0,3},{1,0},{2,1},{3,2},{4,7},{5,4},{6,5},{7,6},{8,11},{9,8},{10,9... | collective-permute-start | bytes 786440 | tf_op jit(solution)/shard_map/ppermute | solution.py:496
  112.1 6.4 %collective-permute-done.21.y1 = bf16[256,512]{1,0:T(8,128)(2,1)S(1)} collective-permute-done((bf16[256,512]{1,0:T(8,128)(2,1)S(1)}, bf16[256,512]{1,0:T(8,128)(2,1)S(1)}, u32[]{:S(2)}, u32[]{:S(2)}) %collective-permute-start.21) | collective-permute-done | bytes 262176 | tf_op jit(solution)/shard_map/ppermute | solution.py:496
  118.9 8.2 %collective-permute-done.23.y2 = bf16[256,512]{1,0:T(8,128)(2,1)S(1)} collective-permute-done((bf16[256,512]{1,0:T(8,128)(2,1)S(1)}, bf16[256,512]{1,0:T(8,128)(2,1)S(1)}, u32[]{:S(2)}, u32[]{:S(2)}) %collective-permute-start.23) | collective-permute-done | bytes 262176 | tf_op jit(solution)/shard_map/ppermute | solution.py:496
  128.1 2.2 %fetch.3.mine = bf16[1024,2048]{1,0:T(8,128)(2,1)S(1)} custom-call(bf16[1024,2048]{1,0:T(8,128)(2,1)} %collective-permute-done.15.w), custom_call_target="tpu_custom_call" | custom-call | tf_op jit(solution)/shard_map/fetch/pallas_call | solution.py:434
  130.4 2.4 %shard_map.115.acc_ref = f32[256,2048]{1,0:T(8,128)S(1)} custom-call(s32[4]{0:T(128)S(1)} %pad_add_fusion.pos, bf16[256,512]{1,0:T(8,128)(2,1)S(1)} %collective-permute-done.21.y1, bf16[256,512]{1,0:T(8,128)(2,1)S(1)} %collective-permute-done.22.y3, bf16[256,512]{1,0:T(8,128)(2,1)S(1)} %collective-permute-done.23.y2, bf16[1024,2048]{1,0:T(8,128)(2,1)S(1)} %fetch.3.mine, ...), custom_call_target="tpu_custom_call" | custom-call | tf_op jit(solution)/shard_map/pallas_call | solution.py:388
  134.1 4.2 %collective-permute-done.14.y2 = bf16[256,512]{1,0:T(8,128)(2,1)S(1)} collective-permute-done((bf16[256,512]{1,0:T(8,128)(2,1)S(1)}, bf16[256,512]{1,0:T(8,128)(2,1)S(1)}, u32[]{:S(2)}, u32[]{:S(2)}) %collective-permute-start.14) | collective-permute-done | bytes 262176 | tf_op jit(solution)/shard_map/ppermute | solution.py:496
  138.3 3.2 %shard_map.116 = bf16[256,2048]{1,0:T(8,128)(2,1)} custom-call(s32[4]{0:T(128)S(1)} %pad_add_fusion.pos, bf16[256,512]{1,0:T(8,128)(2,1)S(1)} %collective-permute-done.12.y1, bf16[256,512]{1,0:T(8,128)(2,1)S(1)} %collective-permute-done.13.y3, bf16[256,512]{1,0:T(8,128)(2,1)S(1)} %collective-permute-done.14.y2, bf16[1024,2048]{1,0:T(8,128)(2,1)S(1)} %fetch.3.mine, ...), custom_call_target="tpu_custom_call" | custom-call | tf_op jit(solution)/shard_map/pallas_call | solution.py:388
  (55 shorter events, 21.1 us)
Async XLA Ops:
  0.0 94.0 %collective-permute-start.15 = (bf16[1024,2048]{1,0:T(8,128)(2,1)}, bf16[1024,2048]{1,0:T(8,128)(2,1)}, u32[]{:S(2)}, u32[]{:S(2)}) collective-permute-start(bf16[1024,2048]{1,0:T(8,128)(2,1)} %w.2), channel_id=1, source_target_pairs={{0,1},{1,2},{2,3},{3,0},{4,7},{5,4},{6,5},{7,6},{8,9},{9,10},{10,1... | collective-permute-start | bytes 12582920 | tf_op jit(solution)/shard_map/ppermute | solution.py:503
  4.4 4.0 %collective-permute-start = (bf16[8,2048]{1,0:T(8,128)(2,1)S(1)}, bf16[8,2048]{1,0:T(8,128)(2,1)S(1)}, u32[]{:S(2)}, u32[]{:S(2)}) collective-permute-start(bf16[8,2048]{1,0:T(8,128)(2,1)S(1)} %rim.1), channel_id=1, source_target_pairs={{0,4},{4,8},{8,12},{12,16},{16,20},{20,24},{24,28},{28,32},{32,36}... | collective-permute-start | bytes 98312 | tf_op jit(solution)/shard_map/ppermute | solution.py:502
  47.8 3.5 %collective-permute-start.1 = (f32[4,128,256]{2,1,0:T(8,128)S(1)}, f32[4,128,256]{2,1,0:T(8,128)S(1)}, u32[]{:S(2)}, u32[]{:S(2)}) collective-permute-start(f32[4,128,256]{2,1,0:T(8,128)S(1)} %get-tuple-element.49), channel_id=1, source_target_pairs={{0,4},{4,0},{8,12},{12,8},{16,20},{20,16},{24,28},{28,24},{32,36},... | collective-permute-start | bytes 1572872 | tf_op jit(solution)/shard_map/ppermute | solution.py:495
  48.6 45.4 %collective-permute-start.16 = (bf16[256,2048]{1,0:T(8,128)(2,1)S(1)}, bf16[256,2048]{1,0:T(8,128)(2,1)S(1)}, u32[]{:S(2)}, u32[]{:S(2)}) collective-permute-start(bf16[256,2048]{1,0:T(8,128)(2,1)S(1)} %quarter.1), channel_id=1, source_target_pairs={{0,2},{1,3},{2,0},{3,1},{4,6},{5,7},{6,4},{7,5},{8,10},{9,11},{10,... | collective-permute-start | bytes 3145736 | tf_op jit(solution)/shard_map/ppermute | solution.py:496
  52.3 7.9 %collective-permute-start.2 = (f32[128,256]{1,0:T(8,128)S(1)}, f32[128,256]{1,0:T(8,128)S(1)}, u32[]{:S(2)}, u32[]{:S(2)}) collective-permute-start(f32[128,256]{1,0:T(8,128)S(1)} %get-tuple-element.55), channel_id=1, source_target_pairs={{0,8},{4,12},{8,16},{12,20},{16,24},{20,28},{24,0},{28,4},{32,40},... | collective-permute-start | bytes 393224 | tf_op jit(solution)/shard_map/ppermute | solution.py:495
  54.5 9.4 %collective-permute-start.3 = (f32[128,256]{1,0:T(8,128)S(1)}, f32[128,256]{1,0:T(8,128)S(1)}, u32[]{:S(2)}, u32[]{:S(2)}) collective-permute-start(f32[128,256]{1,0:T(8,128)S(1)} %get-tuple-element.56), channel_id=1, source_target_pairs={{0,16},{4,20},{8,24},{12,28},{16,0},{20,4},{24,8},{28,12},{32,48},... | collective-permute-start | bytes 393224 | tf_op jit(solution)/shard_map/ppermute | solution.py:495
  57.8 6.1 %collective-permute-start.4 = (f32[128,256]{1,0:T(8,128)S(1)}, f32[128,256]{1,0:T(8,128)S(1)}, u32[]{:S(2)}, u32[]{:S(2)}) collective-permute-start(f32[128,256]{1,0:T(8,128)S(1)} %get-tuple-element.57), channel_id=1, source_target_pairs={{0,24},{4,28},{8,0},{12,4},{16,8},{20,12},{24,16},{28,20},{32,56},... | collective-permute-start | bytes 393224 | tf_op jit(solution)/shard_map/ppermute | solution.py:495
  65.0 5.4 %collective-permute-start.5 = (f32[128,256]{1,0:T(8,128)S(1)}, f32[128,256]{1,0:T(8,128)S(1)}, u32[]{:S(2)}, u32[]{:S(2)}) collective-permute-start(f32[128,256]{1,0:T(8,128)S(1)} %get-tuple-element.63.a0), channel_id=1, source_target_pairs={{0,32},{4,36},{8,40},{12,44},{16,48},{20,52},{24,56},{28,60},{32,6... | collective-permute-start | bytes 393224 | tf_op jit(solution)/shard_map/ppermute | solution.py:495
  66.4 7.4 %collective-permute-start.6 = (f32[128,256]{1,0:T(8,128)S(1)}, f32[128,256]{1,0:T(8,128)S(1)}, u32[]{:S(2)}, u32[]{:S(2)}) collective-permute-start(f32[128,256]{1,0:T(8,128)S(1)} %get-tuple-element.63.a0), channel_id=1, source_target_pairs={{0,64},{4,68},{8,72},{12,76},{16,80},{20,84},{24,88},{28,92},{32,9... | collective-permute-start | bytes 393224 | tf_op jit(solution)/shard_map/ppermute | solution.py:495
  68.9 5.5 %collective-permute-start.7 = (f32[128,256]{1,0:T(8,128)S(1)}, f32[128,256]{1,0:T(8,128)S(1)}, u32[]{:S(2)}, u32[]{:S(2)}) collective-permute-start(f32[128,256]{1,0:T(8,128)S(1)} %get-tuple-element.63.a0), channel_id=1, source_target_pairs={{0,96},{4,100},{8,104},{12,108},{16,112},{20,116},{24,120},{28,124... | collective-permute-start | bytes 393224 | tf_op jit(solution)/shard_map/ppermute | solution.py:495
  75.6 5.5 %collective-permute-start.8 = (f32[128,128]{1,0:T(8,128)S(1)}, f32[128,128]{1,0:T(8,128)S(1)}, u32[]{:S(2)}, u32[]{:S(2)}) collective-permute-start(f32[128,128]{1,0:T(8,128)S(1)} %get-tuple-element.66), channel_id=1, source_target_pairs={{0,8},{4,12},{8,16},{12,20},{16,24},{20,28},{24,0},{28,4},{32,40},... | collective-permute-start | bytes 196616 | tf_op jit(solution)/shard_map/ppermute | solution.py:495
  77.9 5.1 %collective-permute-start.9 = (f32[128,128]{1,0:T(8,128)S(1)}, f32[128,128]{1,0:T(8,128)S(1)}, u32[]{:S(2)}, u32[]{:S(2)}) collective-permute-start(f32[128,128]{1,0:T(8,128)S(1)} %get-tuple-element.67), channel_id=1, source_target_pairs={{0,16},{4,20},{8,24},{12,28},{16,0},{20,4},{24,8},{28,12},{32,48},... | collective-permute-start | bytes 196616 | tf_op jit(solution)/shard_map/ppermute | solution.py:495
  80.6 3.9 %collective-permute-start.10 = (f32[128,128]{1,0:T(8,128)S(1)}, f32[128,128]{1,0:T(8,128)S(1)}, u32[]{:S(2)}, u32[]{:S(2)}) collective-permute-start(f32[128,128]{1,0:T(8,128)S(1)} %get-tuple-element.68), channel_id=1, source_target_pairs={{0,24},{4,28},{8,0},{12,4},{16,8},{20,12},{24,16},{28,20},{32,56},... | collective-permute-start | bytes 196616 | tf_op jit(solution)/shard_map/ppermute | solution.py:495
  85.3 3.5 %collective-permute-start.11 = (f32[4,128,128]{2,1,0:T(8,128)S(1)}, f32[4,128,128]{2,1,0:T(8,128)S(1)}, u32[]{:S(2)}, u32[]{:S(2)}) collective-permute-start(f32[4,128,128]{2,1,0:T(8,128)S(1)} %get-tuple-element.71), channel_id=1, source_target_pairs={{0,4},{4,0},{8,12},{12,8},{16,20},{20,16},{24,28},{28,24},{32,36},... | collective-permute-start | bytes 786440 | tf_op jit(solution)/shard_map/ppermute | solution.py:495
  94.0 36.3 %collective-permute-start.18 = (bf16[1024,2048]{1,0:T(8,128)(2,1)}, bf16[1024,2048]{1,0:T(8,128)(2,1)S(1)}, u32[]{:S(2)}, u32[]{:S(2)}) collective-permute-start(bf16[1024,2048]{1,0:T(8,128)(2,1)} %collective-permute-done.15.w), channel_id=1, source_target_pairs={{0,4},{4,0},{8,12},{12,8},{16,20},{20,16},{24,28},{28,24},{32,36},... | collective-permute-start | bytes 12582920 | tf_op jit(solution)/shard_map/ppermute | solution.py:495
  94.5 13.9 %collective-permute-start.17 = (bf16[256,2048]{1,0:T(8,128)(2,1)S(1)}, bf16[256,2048]{1,0:T(8,128)(2,1)S(1)}, u32[]{:S(2)}, u32[]{:S(2)}) collective-permute-start(bf16[256,2048]{1,0:T(8,128)(2,1)S(1)} %collective-permute-done.16.q_mine), channel_id=1, source_target_pairs={{0,32},{4,12},{8,40},{12,4},{16,48},{20,28},{24,56},{28,20},{32,0}... | collective-permute-start | bytes 3145736 | tf_op jit(solution)/shard_map/ppermute | solution.py:525
  94.5 32.6 %collective-permute-start.19 = (bf16[256,2048]{1,0:T(8,128)(2,1)S(1)}, bf16[256,2048]{1,0:T(8,128)(2,1)S(1)}, u32[]{:S(2)}, u32[]{:S(2)}) collective-permute-start(bf16[256,2048]{1,0:T(8,128)(2,1)S(1)} %collective-permute-done.16.q_mine), channel_id=1, source_target_pairs={{0,4},{4,0},{8,12},{12,8},{16,20},{20,16},{24,28},{28,24},{32,36},... | collective-permute-start | bytes 3145736 | tf_op jit(solution)/shard_map/ppermute | solution.py:495
  108.4 21.9 %collective-permute-start.20 = (bf16[256,2048]{1,0:T(8,128)(2,1)S(1)}, bf16[256,2048]{1,0:T(8,128)(2,1)S(1)}, u32[]{:S(2)}, u32[]{:S(2)}) collective-permute-start(bf16[256,2048]{1,0:T(8,128)(2,1)S(1)} %collective-permute-done.17.n_mine), channel_id=1, source_target_pairs={{0,4},{4,0},{8,12},{12,8},{16,20},{20,16},{24,28},{28,24},{32,36},... | collective-permute-start | bytes 3145736 | tf_op jit(solution)/shard_map/ppermute | solution.py:495
  109.4 9.1 %collective-permute-start.21 = (bf16[256,512]{1,0:T(8,128)(2,1)S(1)}, bf16[256,512]{1,0:T(8,128)(2,1)S(1)}, u32[]{:S(2)}, u32[]{:S(2)}) collective-permute-start(bf16[256,512]{1,0:T(8,128)(2,1)S(1)} %get-tuple-element.83), channel_id=1, source_target_pairs={{0,1},{1,2},{2,3},{3,0},{4,5},{5,6},{6,7},{7,4},{8,9},{9,10},{10,1... | collective-permute-start | bytes 786440 | tf_op jit(solution)/shard_map/ppermute | solution.py:496
  109.4 9.2 %collective-permute-start.22 = (bf16[256,512]{1,0:T(8,128)(2,1)S(1)}, bf16[256,512]{1,0:T(8,128)(2,1)S(1)}, u32[]{:S(2)}, u32[]{:S(2)}) collective-permute-start(bf16[256,512]{1,0:T(8,128)(2,1)S(1)} %get-tuple-element.84), channel_id=1, source_target_pairs={{0,3},{1,0},{2,1},{3,2},{4,7},{5,4},{6,5},{7,6},{8,11},{9,8},{10,9... | collective-permute-start | bytes 786440 | tf_op jit(solution)/shard_map/ppermute | solution.py:496
  118.5 8.6 %collective-permute-start.23 = (bf16[256,512]{1,0:T(8,128)(2,1)S(1)}, bf16[256,512]{1,0:T(8,128)(2,1)S(1)}, u32[]{:S(2)}, u32[]{:S(2)}) collective-permute-start(bf16[256,512]{1,0:T(8,128)(2,1)S(1)} %get-tuple-element.85), channel_id=1, source_target_pairs={{0,2},{1,3},{2,0},{3,1},{4,6},{5,7},{6,4},{7,5},{8,10},{9,11},{10,... | collective-permute-start | bytes 786440 | tf_op jit(solution)/shard_map/ppermute | solution.py:496
  118.6 15.6 %collective-permute-start.12 = (bf16[256,512]{1,0:T(8,128)(2,1)S(1)}, bf16[256,512]{1,0:T(8,128)(2,1)S(1)}, u32[]{:S(2)}, u32[]{:S(2)}) collective-permute-start(bf16[256,512]{1,0:T(8,128)(2,1)S(1)} %get-tuple-element.72), channel_id=1, source_target_pairs={{0,1},{1,2},{2,3},{3,0},{4,5},{5,6},{6,7},{7,4},{8,9},{9,10},{10,1... | collective-permute-start | bytes 786440 | tf_op jit(solution)/shard_map/ppermute | solution.py:496
  127.1 7.1 %collective-permute-start.13 = (bf16[256,512]{1,0:T(8,128)(2,1)S(1)}, bf16[256,512]{1,0:T(8,128)(2,1)S(1)}, u32[]{:S(2)}, u32[]{:S(2)}) collective-permute-start(bf16[256,512]{1,0:T(8,128)(2,1)S(1)} %get-tuple-element.73), channel_id=1, source_target_pairs={{0,3},{1,0},{2,1},{3,2},{4,7},{5,4},{6,5},{7,6},{8,11},{9,8},{10,9... | collective-permute-start | bytes 786440 | tf_op jit(solution)/shard_map/ppermute | solution.py:496
  127.1 11.2 %collective-permute-start.14 = (bf16[256,512]{1,0:T(8,128)(2,1)S(1)}, bf16[256,512]{1,0:T(8,128)(2,1)S(1)}, u32[]{:S(2)}, u32[]{:S(2)}) collective-permute-start(bf16[256,512]{1,0:T(8,128)(2,1)S(1)} %get-tuple-element.74), channel_id=1, source_target_pairs={{0,2},{1,3},{2,0},{3,1},{4,6},{5,7},{6,4},{7,5},{8,10},{9,11},{10,... | collective-permute-start | bytes 786440 | tf_op jit(solution)/shard_map/ppermute | solution.py:496
  (8 other events, 155.5 us)

commit v3 on v2

--- a/solution.py
+++ b/solution.py
@@ -12,7 +12,6 @@
 F32, BF16 = jnp.float32, jnp.bfloat16
 HD = 128
 BLOCK = 64
-KERNEL = 4
 LIMIT = 6 << 20
 
 
@@ -67,13 +66,9 @@
 
 
 def conv(ext, taps):
-    acc = None
-    for j in range(KERNEL):
-        s = KERNEL - 1 - j
-        shifted = ext if s == 0 else pltpu.roll(ext, s, 0)
-        term = taps[j : j + 1] * shifted[8:]
-        acc = term if acc is None else acc + term
-    return silu(acc)
+    older = taps[0:1] * pltpu.roll(ext, 1, 0) + taps[1:2] * ext
+    newer = taps[2:3] * pltpu.roll(ext, 1, 0) + taps[3:4] * ext
+    return silu((pltpu.roll(older, 2, 0) + newer)[8:])
 
 
 def unit(x):
@@ -313,7 +308,7 @@
             ref[:, pl.ds(pl.multiple_of(h * HD, HD), HD)] = y.astype(BF16)
             return 0
 
-        lax.fori_loop(0, per, step, 0)
+        lax.fori_loop(0, per, step, 0, unroll=2)
 
 
 def run_out(pos, base, maps, kept, got, gate, gain, part):

time: 143 us -> 141 us (0.986)
  Pallas kernels: 64.5 us -> 61.1 us
  waiting for transfers between devices: 41.6 us -> 43.5 us
    pallas_call x2, Pallas kernels: 10.3 us -> 6.54 us  [run_out(): pl.pallas_call(functools.partial(out_kernel, part=part), in_specs=[pl.Blo...]
    ppermute x1, waiting for transfers between devices: 6.15 us -> 8.02 us  [shards(): w_far = lax.ppermute(w_near, 'ctx', beside_route(n_ctx))]
  transfers between devices with their start and end apart: 24 -> 24, of which waited for: 15 -> 15; matrix products, arithmetic and copies ran while one was open for 0% -> 0% of each run, Pallas kernels for 43% -> 41%
where the time goes in v3:
time: 141 us; the launch traced here: 140 us
  Pallas kernels  61.1 us (43%)
  waiting for transfers between devices  43.5 us (31%)
  starting transfers between devices  34.9 us (25%)
    pallas_call x1, Pallas kernels, run_scan(): pl.pallas_call(scan_kernel, grid=(rows // BLOCK,), in_specs=[pl.BlockSpec...  39.7 us
    ppermute x14, starting transfers between devices, shards(): send = lambda a, dx, dz, dc: lax.ppermute(a, 'ctx', ctx_route(dx, dz, dc))  21.2 us
    ppermute x7, waiting for transfers between devices, shards(): lax.ppermute(a, 'head', [(i, (i + d) % heads) for i in range(heads)])  20.1 us
    ppermute x14, waiting for transfers between devices, shards(): send = lambda a, dx, dz, dc: lax.ppermute(a, 'ctx', ctx_route(dx, dz, dc))  14.4 us
    ppermute x1, waiting for transfers between devices, shards(): w_far = lax.ppermute(w_near, 'ctx', beside_route(n_ctx))  8.02 us
    ppermute x7, starting transfers between devices, shards(): lax.ppermute(a, 'head', [(i, (i + d) % heads) for i in range(heads)])  7.12 us
    pallas_call x2, Pallas kernels, run_out(): pl.pallas_call(functools.partial(out_kernel, part=part), in_specs=[pl.Blo...  6.54 us
    pallas_call x2, Pallas kernels, project(): pl.pallas_call(functools.partial(project_kernel, part=part, final=final),...  5.52 us
  transfers between devices with their start and end apart: 24, of which 15 were waited for; matrix products, arithmetic and copies ran while one was open for 0% of the time, Pallas kernels for 41%

profile of v3, /device:TPU:1, one launch (start us, length us, event | category | flops | bytes accessed | tf_op | source)
XLA Modules:
  0.0 140.0 jit_solution(6307367952370200600)
XLA Ops:
  0.0 3.6 %collective-permute-start.15 = (bf16[1024,2048]{1,0:T(8,128)(2,1)}, bf16[1024,2048]{1,0:T(8,128)(2,1)}, u32[]{:S(2)}, u32[]{:S(2)}) collective-permute-start(bf16[1024,2048]{1,0:T(8,128)(2,1)} %w.2), channel_id=1, source_target_pairs={{0,1},{1,2},{2,3},{3,0},{4,7},{5,4},{6,5},{7,6},{8,9},{9,10},{10,1... | collective-permute-start | bytes 12582920 | tf_op jit(solution)/shard_map/ppermute | solution.py:498
  4.4 2.9 %collective-permute-start = (bf16[8,2048]{1,0:T(8,128)(2,1)S(1)}, bf16[8,2048]{1,0:T(8,128)(2,1)S(1)}, u32[]{:S(2)}, u32[]{:S(2)}) collective-permute-start(bf16[8,2048]{1,0:T(8,128)(2,1)S(1)} %rim.1), channel_id=1, source_target_pairs={{0,4},{4,8},{8,12},{12,16},{16,20},{20,24},{24,28},{28,32},{32,36}... | collective-permute-start | bytes 98312 | tf_op jit(solution)/shard_map/ppermute | solution.py:497
  8.4 39.7 %scan.1 = (f32[1024,1024]{1,0:T(8,128)S(1)}, bf16[1024,2048]{1,0:T(8,128)(2,1)S(1)}, f32[4,128,256]{2,1,0:T(8,128)S(1)}, f32[4,128,256]{2,1,0:T(8,128)S(1)}) custom-call(s32[4]{0:T(128)S(1)} %pad_add_fusion.pos, bf16[1024,512]{1,0:T(8,128)(2,1)} %q_ref.1, bf16[1024,512]{1,0:T(8,128)(2,1)} %k_ref.1, bf16[1024,1024]{1,0:T(8,128)(2,1)} %v_ref.1, ...), custom_call_target="tpu_custom_call" | custom-call | tf_op jit(solution)/shard_map/scan/pallas_call | solution.py:198
  48.9 3.0 %collective-permute-start.16 = (bf16[256,2048]{1,0:T(8,128)(2,1)S(1)}, bf16[256,2048]{1,0:T(8,128)(2,1)S(1)}, u32[]{:S(2)}, u32[]{:S(2)}) collective-permute-start(bf16[256,2048]{1,0:T(8,128)(2,1)S(1)} %quarter.1), channel_id=1, source_target_pairs={{0,2},{1,3},{2,0},{3,1},{4,6},{5,7},{6,4},{7,5},{8,10},{9,11},{10,... | collective-permute-start | bytes 3145736 | tf_op jit(solution)/shard_map/ppermute | solution.py:491
  52.8 2.0 %collective-permute-start.2 = (f32[128,256]{1,0:T(8,128)S(1)}, f32[128,256]{1,0:T(8,128)S(1)}, u32[]{:S(2)}, u32[]{:S(2)}) collective-permute-start(f32[128,256]{1,0:T(8,128)S(1)} %get-tuple-element.55), channel_id=1, source_target_pairs={{0,8},{4,12},{8,16},{12,20},{16,24},{20,28},{24,0},{28,4},{32,40},... | collective-permute-start | bytes 393224 | tf_op jit(solution)/shard_map/ppermute | solution.py:490
  54.8 3.3 %collective-permute-start.3 = (f32[128,256]{1,0:T(8,128)S(1)}, f32[128,256]{1,0:T(8,128)S(1)}, u32[]{:S(2)}, u32[]{:S(2)}) collective-permute-start(f32[128,256]{1,0:T(8,128)S(1)} %get-tuple-element.56), channel_id=1, source_target_pairs={{0,16},{4,20},{8,24},{12,28},{16,0},{20,4},{24,8},{28,12},{32,48},... | collective-permute-start | bytes 393224 | tf_op jit(solution)/shard_map/ppermute | solution.py:490
  60.5 3.7 %collective-permute-done.3.a2 = f32[128,256]{1,0:T(8,128)S(1)} collective-permute-done((f32[128,256]{1,0:T(8,128)S(1)}, f32[128,256]{1,0:T(8,128)S(1)}, u32[]{:S(2)}, u32[]{:S(2)}) %collective-permute-start.3) | collective-permute-done | bytes 131104 | tf_op jit(solution)/shard_map/ppermute | solution.py:490
  66.8 2.3 %collective-permute-start.6 = (f32[128,256]{1,0:T(8,128)S(1)}, f32[128,256]{1,0:T(8,128)S(1)}, u32[]{:S(2)}, u32[]{:S(2)}) collective-permute-start(f32[128,256]{1,0:T(8,128)S(1)} %get-tuple-element.63.a0), channel_id=1, source_target_pairs={{0,64},{4,68},{8,72},{12,76},{16,80},{20,84},{24,88},{28,92},{32,9... | collective-permute-start | bytes 393224 | tf_op jit(solution)/shard_map/ppermute | solution.py:490
  70.7 3.4 %collective-permute-done.6.a2 = f32[128,256]{1,0:T(8,128)S(1)} collective-permute-done((f32[128,256]{1,0:T(8,128)S(1)}, f32[128,256]{1,0:T(8,128)S(1)}, u32[]{:S(2)}, u32[]{:S(2)}) %collective-permute-start.6) | collective-permute-done | bytes 131104 | tf_op jit(solution)/shard_map/ppermute | solution.py:490
  75.8 2.3 %collective-permute-start.8 = (f32[128,128]{1,0:T(8,128)S(1)}, f32[128,128]{1,0:T(8,128)S(1)}, u32[]{:S(2)}, u32[]{:S(2)}) collective-permute-start(f32[128,128]{1,0:T(8,128)S(1)} %get-tuple-element.66), channel_id=1, source_target_pairs={{0,8},{4,12},{8,16},{12,20},{16,24},{20,28},{24,0},{28,4},{32,40},... | collective-permute-start | bytes 196616 | tf_op jit(solution)/shard_map/ppermute | solution.py:490
  78.1 2.7 %collective-permute-start.9 = (f32[128,128]{1,0:T(8,128)S(1)}, f32[128,128]{1,0:T(8,128)S(1)}, u32[]{:S(2)}, u32[]{:S(2)}) collective-permute-start(f32[128,128]{1,0:T(8,128)S(1)} %get-tuple-element.67), channel_id=1, source_target_pairs={{0,16},{4,20},{8,24},{12,28},{16,0},{20,4},{24,8},{28,12},{32,48},... | collective-permute-start | bytes 196616 | tf_op jit(solution)/shard_map/ppermute | solution.py:490
  81.3 2.0 %collective-permute-done.9.a2 = f32[128,128]{1,0:T(8,128)S(1)} collective-permute-done((f32[128,128]{1,0:T(8,128)S(1)}, f32[128,128]{1,0:T(8,128)S(1)}, u32[]{:S(2)}, u32[]{:S(2)}) %collective-permute-start.9) | collective-permute-done | bytes 65568 | tf_op jit(solution)/shard_map/ppermute | solution.py:490
  85.6 2.3 %collective-permute-start.11 = (f32[4,128,128]{2,1,0:T(8,128)S(1)}, f32[4,128,128]{2,1,0:T(8,128)S(1)}, u32[]{:S(2)}, u32[]{:S(2)}) collective-permute-start(f32[4,128,128]{2,1,0:T(8,128)S(1)} %get-tuple-element.71), channel_id=1, source_target_pairs={{0,4},{4,0},{8,12},{12,8},{16,20},{20,16},{24,28},{28,24},{32,36},... | collective-permute-start | bytes 786440 | tf_op jit(solution)/shard_map/ppermute | solution.py:490
  89.1 3.3 %shard_map.114 = (bf16[256,512]{1,0:T(8,128)(2,1)S(1)}, bf16[256,512]{1,0:T(8,128)(2,1)S(1)}, bf16[256,512]{1,0:T(8,128)(2,1)S(1)}, bf16[256,512]{1,0:T(8,128)(2,1)S(1)}) custom-call(s32[4]{0:T(128)S(1)} %pad_add_fusion.pos, f32[1024,1024]{1,0:T(8,128)S(1)} %get-tuple-element.46.base_ref, bf16[1024,2048]{1,0:T(8,128)(2,1)S(1)} %get-tuple-element.47.map_ref, ...), custom_call_target="tpu_custom_call" | custom-call | tf_op jit(solution)/shard_map/pallas_call | solution.py:318
  94.2 3.3 %shard_map.113 = (bf16[256,512]{1,0:T(8,128)(2,1)S(1)}, bf16[256,512]{1,0:T(8,128)(2,1)S(1)}, bf16[256,512]{1,0:T(8,128)(2,1)S(1)}, bf16[256,512]{1,0:T(8,128)(2,1)S(1)}) custom-call(s32[4]{0:T(128)S(1)} %pad_add_fusion.pos, f32[1024,1024]{1,0:T(8,128)S(1)} %get-tuple-element.46.base_ref, bf16[1024,2048]{1,0:T(8,128)(2,1)S(1)} %get-tuple-element.47.map_ref, ...), custom_call_target="tpu_custom_call" | custom-call | tf_op jit(solution)/shard_map/pallas_call | solution.py:318
  98.8 8.0 %collective-permute-done.17.n_mine = bf16[256,2048]{1,0:T(8,128)(2,1)S(1)} collective-permute-done((bf16[256,2048]{1,0:T(8,128)(2,1)S(1)}, bf16[256,2048]{1,0:T(8,128)(2,1)S(1)}, u32[]{:S(2)}, u32[]{:S(2)}) %collective-permute-start.17) | collective-permute-done | bytes 1048608 | tf_op jit(solution)/shard_map/ppermute | solution.py:520
  107.8 2.7 %collective-permute-start.22 = (bf16[256,512]{1,0:T(8,128)(2,1)S(1)}, bf16[256,512]{1,0:T(8,128)(2,1)S(1)}, u32[]{:S(2)}, u32[]{:S(2)}) collective-permute-start(bf16[256,512]{1,0:T(8,128)(2,1)S(1)} %get-tuple-element.84), channel_id=1, source_target_pairs={{0,3},{1,0},{2,1},{3,2},{4,7},{5,4},{6,5},{7,6},{8,11},{9,8},{10,9... | collective-permute-start | bytes 786440 | tf_op jit(solution)/shard_map/ppermute | solution.py:491
  110.5 6.4 %collective-permute-done.21.y1 = bf16[256,512]{1,0:T(8,128)(2,1)S(1)} collective-permute-done((bf16[256,512]{1,0:T(8,128)(2,1)S(1)}, bf16[256,512]{1,0:T(8,128)(2,1)S(1)}, u32[]{:S(2)}, u32[]{:S(2)}) %collective-permute-start.21) | collective-permute-done | bytes 262176 | tf_op jit(solution)/shard_map/ppermute | solution.py:491
  117.3 8.2 %collective-permute-done.23.y2 = bf16[256,512]{1,0:T(8,128)(2,1)S(1)} collective-permute-done((bf16[256,512]{1,0:T(8,128)(2,1)S(1)}, bf16[256,512]{1,0:T(8,128)(2,1)S(1)}, u32[]{:S(2)}, u32[]{:S(2)}) %collective-permute-start.23) | collective-permute-done | bytes 262176 | tf_op jit(solution)/shard_map/ppermute | solution.py:491
  126.5 2.2 %fetch.3.mine = bf16[1024,2048]{1,0:T(8,128)(2,1)S(1)} custom-call(bf16[1024,2048]{1,0:T(8,128)(2,1)} %collective-permute-done.15.w), custom_call_target="tpu_custom_call" | custom-call | tf_op jit(solution)/shard_map/fetch/pallas_call | solution.py:429
  128.8 2.4 %shard_map.115.acc_ref = f32[256,2048]{1,0:T(8,128)S(1)} custom-call(s32[4]{0:T(128)S(1)} %pad_add_fusion.pos, bf16[256,512]{1,0:T(8,128)(2,1)S(1)} %collective-permute-done.21.y1, bf16[256,512]{1,0:T(8,128)(2,1)S(1)} %collective-permute-done.22.y3, bf16[256,512]{1,0:T(8,128)(2,1)S(1)} %collective-permute-done.23.y2, bf16[1024,2048]{1,0:T(8,128)(2,1)S(1)} %fetch.3.mine, ...), custom_call_target="tpu_custom_call" | custom-call | tf_op jit(solution)/shard_map/pallas_call | solution.py:383
  131.1 1.6 %collective-permute-done.12.y1 = bf16[256,512]{1,0:T(8,128)(2,1)S(1)} collective-permute-done((bf16[256,512]{1,0:T(8,128)(2,1)S(1)}, bf16[256,512]{1,0:T(8,128)(2,1)S(1)}, u32[]{:S(2)}, u32[]{:S(2)}) %collective-permute-start.12) | collective-permute-done | bytes 262176 | tf_op jit(solution)/shard_map/ppermute | solution.py:491
  132.7 4.0 %collective-permute-done.14.y2 = bf16[256,512]{1,0:T(8,128)(2,1)S(1)} collective-permute-done((bf16[256,512]{1,0:T(8,128)(2,1)S(1)}, bf16[256,512]{1,0:T(8,128)(2,1)S(1)}, u32[]{:S(2)}, u32[]{:S(2)}) %collective-permute-start.14) | collective-permute-done | bytes 262176 | tf_op jit(solution)/shard_map/ppermute | solution.py:491
  136.7 3.2 %shard_map.116 = bf16[256,2048]{1,0:T(8,128)(2,1)} custom-call(s32[4]{0:T(128)S(1)} %pad_add_fusion.pos, bf16[256,512]{1,0:T(8,128)(2,1)S(1)} %collective-permute-done.12.y1, bf16[256,512]{1,0:T(8,128)(2,1)S(1)} %collective-permute-done.13.y3, bf16[256,512]{1,0:T(8,128)(2,1)S(1)} %collective-permute-done.14.y2, bf16[1024,2048]{1,0:T(8,128)(2,1)S(1)} %fetch.3.mine, ...), custom_call_target="tpu_custom_call" | custom-call | tf_op jit(solution)/shard_map/pallas_call | solution.py:383
  (55 shorter events, 21.3 us)
Async XLA Ops:
  0.0 92.4 %collective-permute-start.15 = (bf16[1024,2048]{1,0:T(8,128)(2,1)}, bf16[1024,2048]{1,0:T(8,128)(2,1)}, u32[]{:S(2)}, u32[]{:S(2)}) collective-permute-start(bf16[1024,2048]{1,0:T(8,128)(2,1)} %w.2), channel_id=1, source_target_pairs={{0,1},{1,2},{2,3},{3,0},{4,7},{5,4},{6,5},{7,6},{8,9},{9,10},{10,1... | collective-permute-start | bytes 12582920 | tf_op jit(solution)/shard_map/ppermute | solution.py:498
  4.4 4.0 %collective-permute-start = (bf16[8,2048]{1,0:T(8,128)(2,1)S(1)}, bf16[8,2048]{1,0:T(8,128)(2,1)S(1)}, u32[]{:S(2)}, u32[]{:S(2)}) collective-permute-start(bf16[8,2048]{1,0:T(8,128)(2,1)S(1)} %rim.1), channel_id=1, source_target_pairs={{0,4},{4,8},{8,12},{12,16},{16,20},{20,24},{24,28},{28,32},{32,36}... | collective-permute-start | bytes 98312 | tf_op jit(solution)/shard_map/ppermute | solution.py:497
  48.1 3.7 %collective-permute-start.1 = (f32[4,128,256]{2,1,0:T(8,128)S(1)}, f32[4,128,256]{2,1,0:T(8,128)S(1)}, u32[]{:S(2)}, u32[]{:S(2)}) collective-permute-start(f32[4,128,256]{2,1,0:T(8,128)S(1)} %get-tuple-element.49), channel_id=1, source_target_pairs={{0,4},{4,0},{8,12},{12,8},{16,20},{20,16},{24,28},{28,24},{32,36},... | collective-permute-start | bytes 1572872 | tf_op jit(solution)/shard_map/ppermute | solution.py:490
  48.9 43.5 %collective-permute-start.16 = (bf16[256,2048]{1,0:T(8,128)(2,1)S(1)}, bf16[256,2048]{1,0:T(8,128)(2,1)S(1)}, u32[]{:S(2)}, u32[]{:S(2)}) collective-permute-start(bf16[256,2048]{1,0:T(8,128)(2,1)S(1)} %quarter.1), channel_id=1, source_target_pairs={{0,2},{1,3},{2,0},{3,1},{4,6},{5,7},{6,4},{7,5},{8,10},{9,11},{10,... | collective-permute-start | bytes 3145736 | tf_op jit(solution)/shard_map/ppermute | solution.py:491
  52.8 7.7 %collective-permute-start.2 = (f32[128,256]{1,0:T(8,128)S(1)}, f32[128,256]{1,0:T(8,128)S(1)}, u32[]{:S(2)}, u32[]{:S(2)}) collective-permute-start(f32[128,256]{1,0:T(8,128)S(1)} %get-tuple-element.55), channel_id=1, source_target_pairs={{0,8},{4,12},{8,16},{12,20},{16,24},{20,28},{24,0},{28,4},{32,40},... | collective-permute-start | bytes 393224 | tf_op jit(solution)/shard_map/ppermute | solution.py:490
  54.8 9.4 %collective-permute-start.3 = (f32[128,256]{1,0:T(8,128)S(1)}, f32[128,256]{1,0:T(8,128)S(1)}, u32[]{:S(2)}, u32[]{:S(2)}) collective-permute-start(f32[128,256]{1,0:T(8,128)S(1)} %get-tuple-element.56), channel_id=1, source_target_pairs={{0,16},{4,20},{8,24},{12,28},{16,0},{20,4},{24,8},{28,12},{32,48},... | collective-permute-start | bytes 393224 | tf_op jit(solution)/shard_map/ppermute | solution.py:490
  58.1 6.1 %collective-permute-start.4 = (f32[128,256]{1,0:T(8,128)S(1)}, f32[128,256]{1,0:T(8,128)S(1)}, u32[]{:S(2)}, u32[]{:S(2)}) collective-permute-start(f32[128,256]{1,0:T(8,128)S(1)} %get-tuple-element.57), channel_id=1, source_target_pairs={{0,24},{4,28},{8,0},{12,4},{16,8},{20,12},{24,16},{28,20},{32,56},... | collective-permute-start | bytes 393224 | tf_op jit(solution)/shard_map/ppermute | solution.py:490
  65.3 5.4 %collective-permute-start.5 = (f32[128,256]{1,0:T(8,128)S(1)}, f32[128,256]{1,0:T(8,128)S(1)}, u32[]{:S(2)}, u32[]{:S(2)}) collective-permute-start(f32[128,256]{1,0:T(8,128)S(1)} %get-tuple-element.63.a0), channel_id=1, source_target_pairs={{0,32},{4,36},{8,40},{12,44},{16,48},{20,52},{24,56},{28,60},{32,6... | collective-permute-start | bytes 393224 | tf_op jit(solution)/shard_map/ppermute | solution.py:490
  66.8 7.3 %collective-permute-start.6 = (f32[128,256]{1,0:T(8,128)S(1)}, f32[128,256]{1,0:T(8,128)S(1)}, u32[]{:S(2)}, u32[]{:S(2)}) collective-permute-start(f32[128,256]{1,0:T(8,128)S(1)} %get-tuple-element.63.a0), channel_id=1, source_target_pairs={{0,64},{4,68},{8,72},{12,76},{16,80},{20,84},{24,88},{28,92},{32,9... | collective-permute-start | bytes 393224 | tf_op jit(solution)/shard_map/ppermute | solution.py:490
  69.1 5.5 %collective-permute-start.7 = (f32[128,256]{1,0:T(8,128)S(1)}, f32[128,256]{1,0:T(8,128)S(1)}, u32[]{:S(2)}, u32[]{:S(2)}) collective-permute-start(f32[128,256]{1,0:T(8,128)S(1)} %get-tuple-element.63.a0), channel_id=1, source_target_pairs={{0,96},{4,100},{8,104},{12,108},{16,112},{20,116},{24,120},{28,124... | collective-permute-start | bytes 393224 | tf_op jit(solution)/shard_map/ppermute | solution.py:490
  75.8 5.5 %collective-permute-start.8 = (f32[128,128]{1,0:T(8,128)S(1)}, f32[128,128]{1,0:T(8,128)S(1)}, u32[]{:S(2)}, u32[]{:S(2)}) collective-permute-start(f32[128,128]{1,0:T(8,128)S(1)} %get-tuple-element.66), channel_id=1, source_target_pairs={{0,8},{4,12},{8,16},{12,20},{16,24},{20,28},{24,0},{28,4},{32,40},... | collective-permute-start | bytes 196616 | tf_op jit(solution)/shard_map/ppermute | solution.py:490
  78.1 5.1 %collective-permute-start.9 = (f32[128,128]{1,0:T(8,128)S(1)}, f32[128,128]{1,0:T(8,128)S(1)}, u32[]{:S(2)}, u32[]{:S(2)}) collective-permute-start(f32[128,128]{1,0:T(8,128)S(1)} %get-tuple-element.67), channel_id=1, source_target_pairs={{0,16},{4,20},{8,24},{12,28},{16,0},{20,4},{24,8},{28,12},{32,48},... | collective-permute-start | bytes 196616 | tf_op jit(solution)/shard_map/ppermute | solution.py:490
  80.8 3.9 %collective-permute-start.10 = (f32[128,128]{1,0:T(8,128)S(1)}, f32[128,128]{1,0:T(8,128)S(1)}, u32[]{:S(2)}, u32[]{:S(2)}) collective-permute-start(f32[128,128]{1,0:T(8,128)S(1)} %get-tuple-element.68), channel_id=1, source_target_pairs={{0,24},{4,28},{8,0},{12,4},{16,8},{20,12},{24,16},{28,20},{32,56},... | collective-permute-start | bytes 196616 | tf_op jit(solution)/shard_map/ppermute | solution.py:490
  85.6 3.5 %collective-permute-start.11 = (f32[4,128,128]{2,1,0:T(8,128)S(1)}, f32[4,128,128]{2,1,0:T(8,128)S(1)}, u32[]{:S(2)}, u32[]{:S(2)}) collective-permute-start(f32[4,128,128]{2,1,0:T(8,128)S(1)} %get-tuple-element.71), channel_id=1, source_target_pairs={{0,4},{4,0},{8,12},{12,8},{16,20},{20,16},{24,28},{28,24},{32,36},... | collective-permute-start | bytes 786440 | tf_op jit(solution)/shard_map/ppermute | solution.py:490
  92.4 36.3 %collective-permute-start.18 = (bf16[1024,2048]{1,0:T(8,128)(2,1)}, bf16[1024,2048]{1,0:T(8,128)(2,1)S(1)}, u32[]{:S(2)}, u32[]{:S(2)}) collective-permute-start(bf16[1024,2048]{1,0:T(8,128)(2,1)} %collective-permute-done.15.w), channel_id=1, source_target_pairs={{0,4},{4,0},{8,12},{12,8},{16,20},{20,16},{24,28},{28,24},{32,36},... | collective-permute-start | bytes 12582920 | tf_op jit(solution)/shard_map/ppermute | solution.py:490
  92.9 13.9 %collective-permute-start.17 = (bf16[256,2048]{1,0:T(8,128)(2,1)S(1)}, bf16[256,2048]{1,0:T(8,128)(2,1)S(1)}, u32[]{:S(2)}, u32[]{:S(2)}) collective-permute-start(bf16[256,2048]{1,0:T(8,128)(2,1)S(1)} %collective-permute-done.16.q_mine), channel_id=1, source_target_pairs={{0,32},{4,12},{8,40},{12,4},{16,48},{20,28},{24,56},{28,20},{32,0}... | collective-permute-start | bytes 3145736 | tf_op jit(solution)/shard_map/ppermute | solution.py:520
  92.9 32.6 %collective-permute-start.19 = (bf16[256,2048]{1,0:T(8,128)(2,1)S(1)}, bf16[256,2048]{1,0:T(8,128)(2,1)S(1)}, u32[]{:S(2)}, u32[]{:S(2)}) collective-permute-start(bf16[256,2048]{1,0:T(8,128)(2,1)S(1)} %collective-permute-done.16.q_mine), channel_id=1, source_target_pairs={{0,4},{4,0},{8,12},{12,8},{16,20},{20,16},{24,28},{28,24},{32,36},... | collective-permute-start | bytes 3145736 | tf_op jit(solution)/shard_map/ppermute | solution.py:490
  106.8 21.9 %collective-permute-start.20 = (bf16[256,2048]{1,0:T(8,128)(2,1)S(1)}, bf16[256,2048]{1,0:T(8,128)(2,1)S(1)}, u32[]{:S(2)}, u32[]{:S(2)}) collective-permute-start(bf16[256,2048]{1,0:T(8,128)(2,1)S(1)} %collective-permute-done.17.n_mine), channel_id=1, source_target_pairs={{0,4},{4,0},{8,12},{12,8},{16,20},{20,16},{24,28},{28,24},{32,36},... | collective-permute-start | bytes 3145736 | tf_op jit(solution)/shard_map/ppermute | solution.py:490
  107.8 9.1 %collective-permute-start.21 = (bf16[256,512]{1,0:T(8,128)(2,1)S(1)}, bf16[256,512]{1,0:T(8,128)(2,1)S(1)}, u32[]{:S(2)}, u32[]{:S(2)}) collective-permute-start(bf16[256,512]{1,0:T(8,128)(2,1)S(1)} %get-tuple-element.83), channel_id=1, source_target_pairs={{0,1},{1,2},{2,3},{3,0},{4,5},{5,6},{6,7},{7,4},{8,9},{9,10},{10,1... | collective-permute-start | bytes 786440 | tf_op jit(solution)/shard_map/ppermute | solution.py:491
  107.8 9.2 %collective-permute-start.22 = (bf16[256,512]{1,0:T(8,128)(2,1)S(1)}, bf16[256,512]{1,0:T(8,128)(2,1)S(1)}, u32[]{:S(2)}, u32[]{:S(2)}) collective-permute-start(bf16[256,512]{1,0:T(8,128)(2,1)S(1)} %get-tuple-element.84), channel_id=1, source_target_pairs={{0,3},{1,0},{2,1},{3,2},{4,7},{5,4},{6,5},{7,6},{8,11},{9,8},{10,9... | collective-permute-start | bytes 786440 | tf_op jit(solution)/shard_map/ppermute | solution.py:491
  116.9 8.6 %collective-permute-start.23 = (bf16[256,512]{1,0:T(8,128)(2,1)S(1)}, bf16[256,512]{1,0:T(8,128)(2,1)S(1)}, u32[]{:S(2)}, u32[]{:S(2)}) collective-permute-start(bf16[256,512]{1,0:T(8,128)(2,1)S(1)} %get-tuple-element.85), channel_id=1, source_target_pairs={{0,2},{1,3},{2,0},{3,1},{4,6},{5,7},{6,4},{7,5},{8,10},{9,11},{10,... | collective-permute-start | bytes 786440 | tf_op jit(solution)/shard_map/ppermute | solution.py:491
  117.0 15.7 %collective-permute-start.12 = (bf16[256,512]{1,0:T(8,128)(2,1)S(1)}, bf16[256,512]{1,0:T(8,128)(2,1)S(1)}, u32[]{:S(2)}, u32[]{:S(2)}) collective-permute-start(bf16[256,512]{1,0:T(8,128)(2,1)S(1)} %get-tuple-element.72), channel_id=1, source_target_pairs={{0,1},{1,2},{2,3},{3,0},{4,5},{5,6},{6,7},{7,4},{8,9},{9,10},{10,1... | collective-permute-start | bytes 786440 | tf_op jit(solution)/shard_map/ppermute | solution.py:491
  125.5 7.3 %collective-permute-start.13 = (bf16[256,512]{1,0:T(8,128)(2,1)S(1)}, bf16[256,512]{1,0:T(8,128)(2,1)S(1)}, u32[]{:S(2)}, u32[]{:S(2)}) collective-permute-start(bf16[256,512]{1,0:T(8,128)(2,1)S(1)} %get-tuple-element.73), channel_id=1, source_target_pairs={{0,3},{1,0},{2,1},{3,2},{4,7},{5,4},{6,5},{7,6},{8,11},{9,8},{10,9... | collective-permute-start | bytes 786440 | tf_op jit(solution)/shard_map/ppermute | solution.py:491
  125.5 11.2 %collective-permute-start.14 = (bf16[256,512]{1,0:T(8,128)(2,1)S(1)}, bf16[256,512]{1,0:T(8,128)(2,1)S(1)}, u32[]{:S(2)}, u32[]{:S(2)}) collective-permute-start(bf16[256,512]{1,0:T(8,128)(2,1)S(1)} %get-tuple-element.74), channel_id=1, source_target_pairs={{0,2},{1,3},{2,0},{3,1},{4,6},{5,7},{6,4},{7,5},{8,10},{9,11},{10,... | collective-permute-start | bytes 786440 | tf_op jit(solution)/shard_map/ppermute | solution.py:491
  (8 other events, 155.3 us)
